TPU v7x, 512 devices: a whole 4x4x16 slice. The times are simulated.
512 devices in a mesh: gx: 32 (over z_lo, y), gy: 16 (over z_hi, x, core).
Axes of the slice: x: 4, y: 4, z: 16 (z_hi: 2, z_lo: 8; z = z_hi * 8 + z_lo), core: 2. Of those that a mesh axis runs over, the one named last changes fastest.
Arguments:
- vectors: float32 [8, 3, 4, 256, 2048], P(None, None, None, 'gx', 'gy'), may hold values from -2000 to 2000, as said below
- background: float32 [3, 4, 256, 2048], P(None, None, 'gx', 'gy'), may hold values from -1 to 1
- obs_site: int32 [2097152], P(('gx', 'gy')), may hold values from 0 to 12287
- obs_offset: float32 [2, 2097152], P(None, ('gx', 'gy')), may hold values from -1 to 1
- obs_error: float32 [2097152], P(('gx', 'gy')), may hold values from 0.5 to 4
Outputs:
- analysis: float32 [8, 3, 4, 256, 2048], P(None, None, None, 'gx', 'gy')
- obs_perturb: float32 [8, 2097152], P(None, ('gx', 'gy'))
Inputs may be any that keep to these rules, and one draw needn't show every extreme that they name: Drawn with scales that vary over vectors, variables, levels and cells. `obs_site`: observation n lies in the tile of device n // 4096; its site is ((variable * 4 + level) * 8 + row) * 128 + column, with row and column local to that tile.
All inputs are finite; a program needn't handle non-finite values.
Results may differ from a plain program's by a relative error of at most 0.000092.
Values sent between devices are 32-bit elements; how exact they have to be, the bound alone decides.
No kernel may reach another device: no remote copies, remote signals or barrier semaphores. Data moves between devices by JAX's collectives and lax.ppermute only.
A program may use at most 192 MiB of HBM per device.

v0:
```python
import jax
import jax.numpy as jnp
from jax import lax
from jax.sharding import Mesh
from jax.sharding import PartitionSpec as P

L = 4
GX_GY = ("gx_0", "gx_1", "gy_0", "gy_1", "gy_2")
GX = ("gx_0", "gx_1")
GY = ("gy_0", "gy_1", "gy_2")


step_size = 0.35
highest = lax.Precision.HIGHEST


def padded_2(block, sides, width):
    for axis, dim in sides:
        count = lax.axis_size(axis)
        forward = [(i, i + 1) for i in range(count - 1)]
        forward.append((count - 1, 0))
        backward = [(target, source) for source, target in forward]
        low = lax.ppermute(
            lax.slice_in_dim(block, block.shape[dim] - width, None, axis=dim), axis, forward
        )
        high = lax.ppermute(lax.slice_in_dim(block, 0, width, axis=dim), axis, backward)
        block = jnp.concatenate([low, block, high], axis=dim)
    return block


def over_axes(value, axes):
    for axis in axes:
        value = lax.psum(value, axis)
    return value


def trim_rim(field, width):
    return field[..., width : field.shape[-2] - width, width : field.shape[-1] - width]


def tendency(padded, background):

    def along_x(field):
        return 0.5 * (field[..., 2:, 1:-1] - field[..., :-2, 1:-1])

    def along_y(field):
        return 0.5 * (field[..., 1:-1, 2:] - field[..., 1:-1, :-2])

    wind_x, wind_y, vort_abs = (background[0], background[1], background[2])
    east_part = padded[:, 0]
    north_part = padded[:, 1]
    height = padded[:, 2]

    def advect(field):
        return wind_x * along_x(field) + wind_y * along_y(field)

    tend_east = -advect(east_part) - along_x(height) + vort_abs * trim_rim(north_part, 1)
    tend_north = -advect(north_part) - along_y(height) - vort_abs * trim_rim(east_part, 1)
    tend_height = -advect(height) - (along_x(east_part) + along_y(north_part))
    return jnp.stack([tend_east, tend_north, tend_height], axis=1)


def sample(rimmed, obs_site, obs_offset):
    vector_count = rimmed.shape[0]
    rows_dev = rimmed.shape[3] - 2
    cols_dev = rimmed.shape[4] - 2
    windows = []
    for step_x in (-1, 0, 1):
        for step_y in (-1, 0, 1):
            window = rimmed[
                :, :, :, 1 + step_x : 1 + step_x + rows_dev, 1 + step_y : 1 + step_y + cols_dev
            ]
            windows.append(window.reshape(vector_count, -1))
    table = jnp.concatenate(windows, axis=0).T
    picked = jnp.take(table, obs_site, axis=0).reshape(obs_site.shape[0], 9, vector_count)
    shift_x = obs_offset[0]
    shift_y = obs_offset[1]
    weights_x = (jnp.maximum(-shift_x, 0.0), 1.0 - jnp.abs(shift_x), jnp.maximum(shift_x, 0.0))
    weights_y = (jnp.maximum(-shift_y, 0.0), 1.0 - jnp.abs(shift_y), jnp.maximum(shift_y, 0.0))
    pair_weights = jnp.stack(
        [weights_x[i] * weights_y[j] for i in range(3) for j in range(3)], axis=1
    )
    return jnp.einsum(
        "ow,owk->ko", pair_weights, picked, precision=highest, preferred_element_type=jnp.float32
    )


def local(vectors, background, obs_site, obs_offset, obs_error):
    vector_count = vectors.shape[0]
    devices_all = lax.axis_size(GX) * lax.axis_size(GY)
    cells_all = float(3 * L * vectors.shape[3] * vectors.shape[4] * devices_all)
    obs_all = float(obs_site.shape[0] * devices_all)
    identity = jnp.eye(vector_count, dtype=jnp.float32)
    joined = jnp.concatenate([vectors, background[None]], axis=0)
    widened = padded_2(joined, ((GX, 3), (GY, 4)), 4)
    start_rim = widened[:vector_count]
    back_rim = widened[vector_count]
    section_one = trim_rim(start_rim, 1) + step_size * tendency(start_rim, trim_rim(back_rim, 1))
    section_two = 0.75 * trim_rim(start_rim, 2) + 0.25 * (
        trim_rim(section_one, 1) + step_size * tendency(section_one, trim_rim(back_rim, 2))
    )
    bred_rim = trim_rim(start_rim, 3) / 3.0 + 2.0 / 3.0 * (
        trim_rim(section_two, 1) + step_size * tendency(section_two, trim_rim(back_rim, 3))
    )
    bred = trim_rim(bred_rim, 1)
    flattened = bred.reshape(vector_count, -1)
    gram_local = jnp.dot(
        flattened, flattened.T, precision=highest, preferred_element_type=jnp.float32
    )
    projected = sample(bred_rim, obs_site, obs_offset)
    normal_local = jnp.dot(
        projected / obs_error, projected.T, precision=highest, preferred_element_type=jnp.float32
    )
    gram_total, normal_total = (over_axes(gram_local, GX_GY), over_axes(normal_local, GX_GY))
    lower = jnp.linalg.cholesky(gram_total / cells_all)
    inv_lower = lax.linalg.triangular_solve(lower, identity, left_side=True, lower=True)
    system = identity + jnp.dot(
        jnp.dot(inv_lower, normal_total / obs_all, precision=highest),
        inv_lower.T,
        precision=highest,
    )
    factor = jnp.linalg.cholesky(system)
    inv_factor = lax.linalg.triangular_solve(factor, identity, left_side=True, lower=True)
    combo = jnp.dot(inv_factor, inv_lower, precision=highest)
    analysis = jnp.dot(
        combo, flattened, precision=highest, preferred_element_type=jnp.float32
    ).reshape(bred.shape)
    obs_perturb = jnp.dot(
        combo, projected, precision=highest, preferred_element_type=jnp.float32
    ) / jnp.sqrt(obs_error)
    return (analysis, obs_perturb)


def solution(mesh):
    torus = Mesh(mesh.devices.reshape(8, 4, 2, 4, 2), ("gx_0", "gx_1", "gy_0", "gy_1", "gy_2"))
    return jax.shard_map(
        local,
        mesh=torus,
        in_specs=(
            P(None, None, None, GX, GY),
            P(None, None, GX, GY),
            P(GX_GY),
            P(None, GX_GY),
            P(GX_GY),
        ),
        out_specs=(P(None, None, None, GX, GY), P(None, GX_GY)),
        check_vma=False,
    )
```

profile of v0, /device:TPU:1, one launch (start us, length us, event | category | flops | bytes accessed | tf_op | source)
XLA Modules:
  0.0 241.4 jit_solution(10379105029754994762)
XLA Ops:
  0.7 1.3 copy.55
  1.9 0.8 fusion.18
  2.7 4.0 %collective-permute-start = (f32[9,3,4,4,128]{4,0,3,2,1:T(8,128)S(1)}, f32[9,3,4,4,128]{4,0,3,2,1:T(8,128)S(1)}, u32[]{:S(2)}, u32[]{:S(2)}) collective-permute-start(f32[9,3,4,4,128]{4,0,3,2,1:T(8,128)S(1)} %get-tuple-element.48), channel_id=1, source_target_pairs={{0,16},{16,32},{32,48},{48,64},{64,80},{80,96},{96,112},{112,128},... | collective-permute-start | bytes 663560 | tf_op jit(solution)/shard_map/ppermute | solution.py:23
  6.8 14.0 %collective-permute-start.1 = (f32[9,3,4,4,128]{4,0,3,2,1:T(8,128)S(1)}, f32[9,3,4,4,128]{4,0,3,2,1:T(8,128)S(1)}, u32[]{:S(2)}, u32[]{:S(2)}) collective-permute-start(f32[9,3,4,4,128]{4,0,3,2,1:T(8,128)S(1)} %get-tuple-element.49), channel_id=1, source_target_pairs={{16,0},{32,16},{48,32},{64,48},{80,64},{96,80},{112,96},{128,112},... | collective-permute-start | bytes 663560 | tf_op jit(solution)/shard_map/ppermute | solution.py:26
  20.8 0.8 multiply_bitcast_fusion
  22.2 3.1 %collective-permute-done = f32[9,3,4,4,128]{4,0,3,2,1:T(8,128)S(1)} collective-permute-done((f32[9,3,4,4,128]{4,0,3,2,1:T(8,128)S(1)}, f32[9,3,4,4,128]{4,0,3,2,1:T(8,128)S(1)}, u32[]{:S(2)}, u32[]{:S(2)}) %collective-permute-start) | collective-permute-done | bytes 221216 | tf_op jit(solution)/shard_map/ppermute | solution.py:23
  25.3 0.9 collective-permute-done.1
  26.2 0.7 copy-done.2
  27.7 1.5 copy.56
  29.2 7.0 %collective-permute-start.2 = (f32[9,3,4,16,4]{3,4,2,1,0:T(4,128)}, f32[9,3,4,16,4]{3,4,2,1,0:T(4,128)S(1)}, u32[]{:S(2)}, u32[]{:S(2)}) collective-permute-start(f32[9,3,4,16,4]{3,4,2,1,0:T(4,128)} %copy.56), channel_id=1, source_target_pairs={{0,1},{1,2},{2,3},{3,4},{4,5},{5,6},{6,7},{7,8},{8,9},{9,10},{10,1... | collective-permute-start | bytes 82952 | tf_op jit(solution)/shard_map/ppermute | solution.py:23
  36.2 0.8 copy.57
  37.1 2.1 collective-permute-start.3
  39.9 1.5 stack.60
  41.4 0.8 copy.58
  42.2 2.2 collective-permute-done.3
  44.4 1.8 copy.59
  46.2 1.7 pad_maximum_fusion.3
  49.0 1.3 pad_maximum_fusion
  50.5 0.8 subtract_bitcast_fusion
  51.3 1.4 fusion.13
  53.2 0.7 subtract_bitcast_fusion.1
  53.8 1.2 fusion.26
  55.0 0.8 fusion.1
  56.5 1.0 fusion.40
  58.1 1.7 fusion.75
  59.8 1.3 convolution_bitcast_fusion
  61.0 4.8 %copy.63 = f32[8,12288]{0,1:T(8,128)} copy(f32[8,12288]{1,0:T(8,128)} %bitcast.145) | data formatting | bytes 786432 | tf_op jit(solution)/shard_map/reshape | solution.py:73
  65.9 4.8 %copy.64 = f32[8,12288]{0,1:T(8,128)} copy(f32[8,12288]{1,0:T(8,128)} %bitcast.144) | data formatting | bytes 786432 | tf_op jit(solution)/shard_map/reshape | solution.py:73
  70.7 4.8 %copy.65 = f32[8,12288]{0,1:T(8,128)} copy(f32[8,12288]{1,0:T(8,128)} %bitcast.143) | data formatting | bytes 786432 | tf_op jit(solution)/shard_map/reshape | solution.py:73
  75.4 3.9 %copy.66 = f32[8,12288]{0,1:T(8,128)} copy(f32[8,12288]{1,0:T(8,128)S(1)} %bitcast.142) | data formatting | bytes 786432 | tf_op jit(solution)/shard_map/reshape | solution.py:73
  79.4 4.0 %copy.67 = f32[8,12288]{0,1:T(8,128)} copy(f32[8,12288]{1,0:T(8,128)S(1)} %bitcast.141) | data formatting | bytes 786432 | tf_op jit(solution)/shard_map/reshape | solution.py:106
  83.3 3.9 %copy.68 = f32[8,12288]{0,1:T(8,128)} copy(f32[8,12288]{1,0:T(8,128)S(1)} %bitcast.140) | data formatting | bytes 786432 | tf_op jit(solution)/shard_map/reshape | solution.py:73
  87.2 3.9 %copy.69 = f32[8,12288]{0,1:T(8,128)} copy(f32[8,12288]{1,0:T(8,128)S(1)} %bitcast.139) | data formatting | bytes 786432 | tf_op jit(solution)/shard_map/reshape | solution.py:73
  91.2 3.9 %copy.70 = f32[8,12288]{0,1:T(8,128)} copy(f32[8,12288]{1,0:T(8,128)S(1)} %bitcast.138) | data formatting | bytes 786432 | tf_op jit(solution)/shard_map/reshape | solution.py:73
  95.0 3.9 %copy.71 = f32[8,12288]{0,1:T(8,128)} copy(f32[8,12288]{1,0:T(8,128)S(1)} %bitcast.137) | data formatting | bytes 786432 | tf_op jit(solution)/shard_map/reshape | solution.py:73
  98.9 34.1 %concatenate.15 = f32[72,12288]{0,1:T(8,128)} concatenate(f32[8,12288]{0,1:T(8,128)} %copy.63, f32[8,12288]{0,1:T(8,128)} %copy.64, f32[8,12288]{0,1:T(8,128)} %copy.65, f32[8,12288]{0,1:T(8,128)} %copy.66, f32[8,12288]{0,1:T(8,128)} %copy.67, f32[8,12288]{0,1:T(8,128)} %copy.68, f32[8,12288]{0,1:T(8,128)} %copy.69, f32[8,12288]{0,1:T(8,128)} %copy.70, f32[8,12288]{0,1:T(8,128)} %copy.71), dimensions={0} | concatenate | bytes 7077888 | tf_op jit(solution)/shard_map/concatenate | solution.py:74
  133.1 13.6 %gather_fusion = f32[4096,72]{1,0:T(8,128)S(1)} fusion(f32[12288,72]{1,0:T(8,128)} %bitcast.133, s32[4096]{0:T(1024)S(1)} %copy-done.17), kind=kCustom, calls=%fused_computation | custom fusion | bytes 2375680 | tf_op jit(solution)/shard_map/jit(_take)/gather | solution.py:75
  146.7 1.7 copy.72
  148.3 1.4 fusion.3
  150.1 23.0 %all-reduce = (f32[8,8]{0,1:T(8,128)S(1)}, f32[8,8]{1,0:T(8,128)S(1)}) all-reduce(f32[8,8]{0,1:T(8,128)S(1)} %convolution_bitcast_fusion, f32[8,8]{1,0:T(8,128)S(1)} %fusion.45), channel_id=1, replica_groups=mesh['gx_0'=8,'gx_1'=4,'gy_0'=2,'gy_1'=4,'gy_2'=2] {'gx_0'}, use_global_device_ids=true, to_apply=%region_0.1 | all-reduce | flops 128 | bytes 1024 | tf_op jit(solution)/shard_map/psum | solution.py:33
  173.1 16.6 %all-reduce.2 = (f32[8,8]{0,1:T(8,128)S(1)}, f32[8,8]{1,0:T(8,128)S(1)}) all-reduce(f32[8,8]{0,1:T(8,128)S(1)} %get-tuple-element.12, f32[8,8]{1,0:T(8,128)S(1)} %get-tuple-element.13), channel_id=1, replica_groups=mesh['gx_0'=8,'gx_1'=4,'gy_0'=2,'gy_1'=4,'gy_2'=2] {'gx_1'}, use_global_device_ids=true, to_apply=%region_1.2 | all-reduce | flops 128 | bytes 1024 | tf_op jit(solution)/shard_map/psum | solution.py:33
  189.7 12.6 %all-reduce.4 = (f32[8,8]{0,1:T(8,128)S(1)}, f32[8,8]{1,0:T(8,128)S(1)}) all-reduce(f32[8,8]{0,1:T(8,128)S(1)} %get-tuple-element.16, f32[8,8]{1,0:T(8,128)S(1)} %get-tuple-element.17), channel_id=1, replica_groups=mesh['gx_0'=8,'gx_1'=4,'gy_0'=2,'gy_1'=4,'gy_2'=2] {'gy_0'}, use_global_device_ids=true, to_apply=%region_2.3 | all-reduce | flops 128 | bytes 1024 | tf_op jit(solution)/shard_map/psum | solution.py:33
  202.3 28.0 %all-reduce.1 = (f32[8,8]{0,1:T(8,128)S(1)}, f32[8,8]{1,0:T(8,128)S(1)}) all-reduce(f32[8,8]{0,1:T(8,128)S(1)} %get-tuple-element.20, f32[8,8]{1,0:T(8,128)S(1)} %get-tuple-element.21), channel_id=1, replica_groups=mesh['gx_0'=8,'gx_1'=4,'gy_0'=2,'gy_1'=4,'gy_2'=2] {'gy_1'}, use_global_device_ids=true, to_apply=%region_3.4 | all-reduce | flops 128 | bytes 1024 | tf_op jit(solution)/shard_map/psum | solution.py:33
  230.3 2.5 %all-reduce.3 = (f32[8,8]{0,1:T(8,128)S(1)}, f32[8,8]{1,0:T(8,128)S(1)}) all-reduce(f32[8,8]{0,1:T(8,128)S(1)} %get-tuple-element.14, f32[8,8]{1,0:T(8,128)S(1)} %get-tuple-element.15), channel_id=1, replica_groups=mesh['gx_0'=8,'gx_1'=4,'gy_0'=2,'gy_1'=4,'gy_2'=2] {'gy_2'}, use_global_device_ids=true, to_apply=%region_4.5 | all-reduce | flops 128 | bytes 1024 | tf_op jit(solution)/shard_map/psum | solution.py:33
  232.9 0.7 cholesky.44
  236.1 0.7 cholesky.55
  239.7 0.9 convolution_divide_fusion
  240.6 0.8 copy.76
  (79 shorter events, 10.8 us)
Async XLA Ops:
  0.6 26.3 %copy-start.5 = (f32[3,4,8,128]{3,2,1,0:T(8,128)S(1)}, f32[3,4,8,128]{3,2,1,0:T(8,128)}, u32[]{:S(2)}) copy-start(f32[3,4,8,128]{3,2,1,0:T(8,128)} %param.9) | copy-start | bytes 147460
  0.6 20.2 %copy-start.18 = (f32[2,4096]{1,0:T(2,128)S(1)}, f32[2,4096]{1,0:T(2,128)}, u32[]{:S(2)}) copy-start(f32[2,4096]{1,0:T(2,128)} %param.11) | copy-start | bytes 98308
  0.7 21.0 %copy-start.7 = (s32[4096]{0:T(1024)S(1)}, s32[4096]{0:T(1024)}, u32[]{:S(2)}) copy-start(s32[4096]{0:T(1024)} %param.10) | copy-start | bytes 49156
  2.7 22.6 %collective-permute-start = (f32[9,3,4,4,128]{4,0,3,2,1:T(8,128)S(1)}, f32[9,3,4,4,128]{4,0,3,2,1:T(8,128)S(1)}, u32[]{:S(2)}, u32[]{:S(2)}) collective-permute-start(f32[9,3,4,4,128]{4,0,3,2,1:T(8,128)S(1)} %get-tuple-element.48), channel_id=1, source_target_pairs={{0,16},{16,32},{32,48},{48,64},{64,80},{80,96},{96,112},{112,128},... | collective-permute-start | bytes 663560 | tf_op jit(solution)/shard_map/ppermute | solution.py:23
  6.8 19.5 %collective-permute-start.1 = (f32[9,3,4,4,128]{4,0,3,2,1:T(8,128)S(1)}, f32[9,3,4,4,128]{4,0,3,2,1:T(8,128)S(1)}, u32[]{:S(2)}, u32[]{:S(2)}) collective-permute-start(f32[9,3,4,4,128]{4,0,3,2,1:T(8,128)S(1)} %get-tuple-element.49), channel_id=1, source_target_pairs={{16,0},{32,16},{48,32},{64,48},{80,64},{96,80},{112,96},{128,112},... | collective-permute-start | bytes 663560 | tf_op jit(solution)/shard_map/ppermute | solution.py:26
  25.3 0.9 copy-start
  26.2 0.7 copy-start.2
  29.1 10.6 %copy-start.20 = (f32[4096]{0:T(1024)S(1)}, f32[4096]{0:T(1024)}, u32[]{:S(2)}) copy-start(f32[4096]{0:T(1024)} %param.12) | copy-start | bytes 49156
  29.1 10.6 %copy-start.8 = (f32[4096,1]{0,1:T(1,128)S(1)}, f32[4096,1]{0,1:T(1,128)}, u32[]{:S(2)}) copy-start(f32[4096,1]{0,1:T(1,128)} %get-tuple-element.59) | copy-start | bytes 49156
  29.1 10.7 %copy-start.9 = (f32[4096,1]{0,1:T(1,128)S(1)}, f32[4096,1]{0,1:T(1,128)}, u32[]{:S(2)}) copy-start(f32[4096,1]{0,1:T(1,128)} %get-tuple-element.60) | copy-start | bytes 49156
  29.1 10.7 %copy-start.10 = (f32[4096,1]{0,1:T(1,128)S(1)}, f32[4096,1]{0,1:T(1,128)}, u32[]{:S(2)}) copy-start(f32[4096,1]{0,1:T(1,128)} %get-tuple-element.61) | copy-start | bytes 49156
  29.1 10.7 %copy-start.11 = (f32[4096,1]{0,1:T(1,128)S(1)}, f32[4096,1]{0,1:T(1,128)}, u32[]{:S(2)}) copy-start(f32[4096,1]{0,1:T(1,128)} %get-tuple-element.62) | copy-start | bytes 49156
  29.1 10.7 %copy-start.12 = (f32[4096,1]{0,1:T(1,128)S(1)}, f32[4096,1]{0,1:T(1,128)}, u32[]{:S(2)}) copy-start(f32[4096,1]{0,1:T(1,128)} %get-tuple-element.63) | copy-start | bytes 49156
  29.2 10.7 %copy-start.13 = (f32[4096,1]{0,1:T(1,128)S(1)}, f32[4096,1]{0,1:T(1,128)}, u32[]{:S(2)}) copy-start(f32[4096,1]{0,1:T(1,128)} %get-tuple-element.64) | copy-start | bytes 49156
  29.2 10.7 %copy-start.14 = (f32[4096,1]{0,1:T(1,128)S(1)}, f32[4096,1]{0,1:T(1,128)}, u32[]{:S(2)}) copy-start(f32[4096,1]{0,1:T(1,128)} %get-tuple-element.65) | copy-start | bytes 49156
  29.2 10.7 %copy-start.15 = (f32[4096,1]{0,1:T(1,128)S(1)}, f32[4096,1]{0,1:T(1,128)}, u32[]{:S(2)}) copy-start(f32[4096,1]{0,1:T(1,128)} %get-tuple-element.66) | copy-start | bytes 49156
  29.2 10.7 %copy-start.16 = (f32[4096,1]{0,1:T(1,128)S(1)}, f32[4096,1]{0,1:T(1,128)}, u32[]{:S(2)}) copy-start(f32[4096,1]{0,1:T(1,128)} %get-tuple-element.67) | copy-start | bytes 49156
  29.2 12.2 %collective-permute-start.2 = (f32[9,3,4,16,4]{3,4,2,1,0:T(4,128)}, f32[9,3,4,16,4]{3,4,2,1,0:T(4,128)S(1)}, u32[]{:S(2)}, u32[]{:S(2)}) collective-permute-start(f32[9,3,4,16,4]{3,4,2,1,0:T(4,128)} %copy.56), channel_id=1, source_target_pairs={{0,1},{1,2},{2,3},{3,4},{4,5},{5,6},{6,7},{7,8},{8,9},{9,10},{10,1... | collective-permute-start | bytes 82952 | tf_op jit(solution)/shard_map/ppermute | solution.py:23
  37.1 7.3 %collective-permute-start.3 = (f32[9,3,4,16,4]{3,4,2,1,0:T(4,128)S(1)}, f32[9,3,4,16,4]{3,4,2,1,0:T(4,128)}, u32[]{:S(2)}, u32[]{:S(2)}) collective-permute-start(f32[9,3,4,16,4]{3,4,2,1,0:T(4,128)S(1)} %copy.57), channel_id=1, source_target_pairs={{1,0},{2,1},{3,2},{4,3},{5,4},{6,5},{7,6},{8,7},{9,8},{10,9},{11,1... | collective-permute-start | bytes 82952 | tf_op jit(solution)/shard_map/ppermute | solution.py:26
  47.9 1.0 copy-start.1
  47.9 1.1 copy-start.3
  47.9 1.1 copy-start.6
  98.9 34.1 %copy-start.17 = (s32[4096]{0:T(1024)S(1)}, s32[4096]{0:T(1024)}, u32[]{:S(2)}) copy-start(s32[4096]{0:T(1024)} %fusion.54) | copy-start | bytes 49156
  146.6 1.7 copy-start.4
  146.6 1.7 copy-start.19
  148.3 1.4 copy-start.21
where the time goes:
time: 243 us; the launch traced here: 241 us
  local copies, waits for them, and re-layouts  100 us (41%)
  blocking collectives  82.7 us (34%)
  starting transfers between devices  27.2 us (11%)
  other arithmetic  20.5 us (8%)
  waiting for transfers between devices  6.19 us (3%)
  matrix products  3.89 us (2%)
    psum x5, blocking collectives, over_axes(): value = lax.psum(value, axis)  82.7 us
    concatenate x1, local copies, waits for them, and re-layouts, sample(): table = jnp.concatenate(windows, axis=0).T  34.1 us
    reshape x8, local copies, waits for them, and re-layouts, sample(): windows.append(window.reshape(vector_count, -1))  33.9 us
    ppermute x2, starting transfers between devices, padded_2(): lax.ppermute(lax.slice_in_dim(block, 0, width, axis=dim), axis, backward)  16.1 us
    gather x2, local copies, waits for them, and re-layouts, sample(): jnp.take(table, obs_site, axis=0)  15.2 us
    ppermute x2, starting transfers between devices, padded_2(): lax.ppermute(lax.slice_in_dim(block, block.shape[dim] - width, None, axis...  11.1 us
    another operation x6, other arithmetic, tendency(): return jnp.stack([tend_east, tend_north, tend_height], axis=1)  5.62 us
  transfers between devices with their start and end apart: 4, of which 3 were waited for; matrix products, arithmetic and copies ran while one was open for 2% of the time, Pallas kernels for 0%

commit v1 on v0

v1 whole, which is shorter than its diff:
```python
import functools

import jax
import jax.numpy as jnp
from jax import lax
from jax.experimental import pallas as pl
from jax.experimental.pallas import tpu as pltpu
from jax.sharding import Mesh
from jax.sharding import PartitionSpec as P

K = 8
L = 4
PLANES = 3 * L
ROWS = 8
COLS = 128
OBS = 4096
GX = ("z_lo", "y")
GY = ("z_hi", "x", "core")
GX_GY = GX + GY
FLAT = ("y", "x", "core")
DEEP = ("z_lo", "z_hi")
FIELDS = K * PLANES + PLANES
HALF = FIELDS // 2
GROUPS = 4
PER_GROUP = FIELDS // GROUPS
CHUNK = 256
BATCH = 2
STEP = 0.35
F32 = jnp.float32
highest = lax.Precision.HIGHEST


def iota(shape, dim):
    return lax.broadcasted_iota(jnp.int32, shape, dim)


def roll(x, shift, axis):
    axis = axis % x.ndim
    shift = shift % x.shape[axis]
    return x if shift == 0 else pltpu.roll(x, shift, axis)


def odd_row():
    return lax.rem(lax.axis_index("y"), 2) == 1


def odd_col():
    return lax.axis_index("core") == 1


def pack_rows_kernel(vec_ref, back_ref, one_ref, two_ref, all_ref):
    odd = odd_row()
    all_ref[0 : K * PLANES] = vec_ref[...]
    all_ref[K * PLANES : FIELDS] = back_ref[...]
    first = all_ref[0:HALF]
    second = roll(all_ref[HALF:FIELDS], 4, 1)
    top = iota((HALF, ROWS, COLS), 1) < 4
    down = jnp.where(top, first, second)
    up = jnp.where(top, second, first)
    one_ref[...] = jnp.where(odd, down, up)
    two_ref[...] = jnp.where(odd, up, down)


def pack_cols_kernel(vec_ref, back_ref, got_one, got_two, ext_ref, one_ref, two_ref):
    at_odd_row = odd_row()
    at_odd_col = odd_col()
    ext_ref[0 : K * PLANES, 0:ROWS] = vec_ref[...]
    ext_ref[K * PLANES : FIELDS, 0:ROWS] = back_ref[...]
    top = iota((HALF, ROWS, COLS), 1) < 4
    low = jnp.where(at_odd_row, got_one[...], got_two[...])
    high = jnp.where(at_odd_row, got_two[...], got_one[...])
    ext_ref[0:HALF, ROWS : 2 * ROWS] = jnp.where(top, high, low)
    ext_ref[HALF:FIELDS, ROWS : 2 * ROWS] = roll(jnp.where(top, low, high), 4, 1)
    lane = iota((2 * ROWS, COLS), 1)
    for group in range(GROUPS):
        up = jnp.zeros((2 * ROWS, COLS), F32)
        down = jnp.zeros((2 * ROWS, COLS), F32)
        for m in range(PER_GROUP):
            moved = roll(ext_ref[group * PER_GROUP + m], 4 * m, 1)
            down = jnp.where(lane // 4 == m, moved, down)
            up = jnp.where(lane // 4 == (m + 31) % 32, moved, up)
        one_ref[group] = jnp.where(at_odd_col, down, up)
        two_ref[group] = jnp.where(at_odd_col, up, down)


def tendency(state, back):
    wind_x, wind_y, vort = back
    east, north, height = state

    def along_x(f):
        return 0.5 * (roll(f, -1, f.ndim - 2) - roll(f, 1, f.ndim - 2))

    def along_y(f):
        return 0.5 * (roll(f, -1, f.ndim - 1) - roll(f, 1, f.ndim - 1))

    ex, nx, hx = along_x(east), along_x(north), along_x(height)
    ey, ny, hy = along_y(east), along_y(north), along_y(height)
    tend_east = -(wind_x * ex + wind_y * ey) - hx + vort * north
    tend_north = -(wind_x * nx + wind_y * ny) - hy - vort * east
    tend_height = -(wind_x * hx + wind_y * hy) - (ex + ny)
    return tend_east, tend_north, tend_height


def advance(start, back):
    one = [s + STEP * t for s, t in zip(start, tendency(start, back))]
    two = [
        0.75 * s + 0.25 * (o + STEP * t) for s, o, t in zip(start, one, tendency(one, back))
    ]
    return [
        s / 3.0 + 2.0 / 3.0 * (w + STEP * t) for s, w, t in zip(start, two, tendency(two, back))
    ]


def main_kernel(
    ext_ref, got_one, got_two, site_ref, off_ref, err_ref,
    bred_ref, scaled_ref, sums_ref,
    side_ref, rows_ref, edge_ref, table_ref, pair_ref,
):
    at_odd_col = odd_col()
    lane = iota((2 * ROWS, COLS), 1)
    for group in range(GROUPS):
        left = jnp.where(at_odd_col, got_one[group], got_two[group])
        right = jnp.where(at_odd_col, got_two[group], got_one[group])
        for m in range(PER_GROUP):
            moved = jnp.where(lane < 4, roll(right, -4 * m, 1), roll(left, -4 * m, 1))
            moved = jnp.where((lane < 4) | (lane >= COLS - 4), moved, 0.0)
            side_ref[group * PER_GROUP + m] = moved

    rows_ref[:, PLANES * ROWS + 2 * PLANES :, :] = jnp.zeros((K, COLS - 10 * PLANES, COLS), F32)
    edge_ref[:, PLANES * ROWS + 2 * PLANES :, :] = jnp.zeros((K, COLS - 10 * PLANES, COLS), F32)
    for level in range(L):
        base = K * PLANES + level
        back = [
            jnp.concatenate([ext_ref[base + c * L], side_ref[base + c * L]], axis=-1)[None]
            for c in range(3)
        ]

        def body(i, carry, level=level, back=back):
            start = []
            for c in range(3):
                parts = []
                for b in range(BATCH):
                    at = (i * BATCH + b) * PLANES + c * L + level
                    parts.append(jnp.concatenate([ext_ref[at], side_ref[at]], axis=-1)[None])
                start.append(jnp.concatenate(parts, axis=0))
            done = advance(start, back)
            for c in range(3):
                plane = c * L + level
                for b in range(BATCH):
                    k = i * BATCH + b
                    field = done[c][b]
                    main, side = field[:, :COLS], field[:, COLS:]
                    bred_ref[k * PLANES + plane] = main[:ROWS]
                    for ref, part in ((rows_ref, main), (edge_ref, side)):
                        ref[k, plane * ROWS : (plane + 1) * ROWS] = part[:ROWS]
                        at = PLANES * ROWS + plane
                        ref[k, at : at + 1] = part[2 * ROWS - 1 :]
                        at = PLANES * ROWS + PLANES + plane
                        ref[k, at : at + 1] = part[ROWS : ROWS + 1]
            return carry

        lax.fori_loop(0, K // BATCH, body, 0)

    for i in range(K):
        mine = bred_ref[i * PLANES : (i + 1) * PLANES]
        for j in range(i, K):
            other = mine if i == j else bred_ref[j * PLANES : (j + 1) * PLANES]
            row = jnp.sum(jnp.sum(mine * other, axis=0), axis=0, keepdims=True)
            pair_ref[i * K + j : i * K + j + 1] = row
            if i != j:
                pair_ref[j * K + i : j * K + i + 1] = row
    pair_ref[K * K :] = jnp.zeros((COLS - K * K, COLS), F32)
    contract_last = (((1,), (1,)), ((), ()))
    gram_row = lax.dot_general(
        jnp.ones((8, COLS), F32), pair_ref[...], contract_last,
        precision=highest, preferred_element_type=F32,
    )[0:1]

    def put(at, count, value):
        high = value.astype(jnp.bfloat16)
        low = (value - high.astype(F32)).astype(jnp.bfloat16)
        table_ref[at : at + count, 0:COLS] = high
        table_ref[at : at + count, COLS : 2 * COLS] = low

    ends = jnp.zeros((COLS, COLS), F32)
    lane = iota((COLS, COLS), 1)
    for k in range(K):
        put(k * COLS, COLS, rows_ref[k].T)
        edge = edge_ref[k]
        ends = jnp.where(lane == k, roll(edge, k + 1, 1), ends)
        ends = jnp.where(lane == K + k, roll(edge, K + k, 1), ends)
    put(K * COLS, 2 * K, ends.T[: 2 * K])

    def sample(step, carry):
        at = pl.multiple_of(step * CHUNK, CHUNK)
        site = site_ref[:, pl.ds(at, CHUNK)]
        shift_x = off_ref[0:1, pl.ds(at, CHUNK)]
        shift_y = off_ref[1:2, pl.ds(at, CHUNK)]
        row_at = site // COLS
        plane = site // (ROWS * COLS)
        row = row_at % ROWS
        col = site % COLS
        size_x = jnp.abs(shift_x)
        size_y = jnp.abs(shift_y)
        before = jnp.where(row == 0, PLANES * ROWS + plane, row_at - 1)
        after = jnp.where(row == ROWS - 1, PLANES * ROWS + PLANES + plane, row_at + 1)
        beside = jnp.where(shift_x < 0.0, before, after)
        next_col = jnp.where(shift_y < 0.0, col - 1, col + 1)
        own_x = 1.0 - size_x
        own_y = 1.0 - size_y

        def split(value):
            high = value.astype(jnp.bfloat16).astype(F32)
            return high, value - high

        own_high, own_low = split(own_x)
        side_high, side_low = split(size_x)
        index = iota((COLS, CHUNK), 0)
        at_own = index == row_at
        at_side = index == beside
        pick_high = jnp.where(at_own, own_high, jnp.where(at_side, side_high, 0.0))
        pick_low = jnp.where(at_own, own_low, jnp.where(at_side, side_low, 0.0))
        pick_high = pick_high.astype(jnp.bfloat16)
        pick_low = pick_low.astype(jnp.bfloat16)
        weight = jnp.where(index == col, own_y, jnp.where(index == next_col, size_y, 0.0))
        high2 = jnp.concatenate([pick_high, pick_high], axis=0)
        low2 = jnp.concatenate([pick_low, pick_low], axis=0)

        def mixed(start, count):
            part = table_ref[start : start + count]
            return jnp.dot(part, high2, preferred_element_type=F32) + jnp.dot(
                part, low2, preferred_element_type=F32
            )

        out = jnp.zeros((K, CHUNK), F32)
        sub = iota((K, CHUNK), 0)
        for k in range(K):
            line = jnp.sum(mixed(k * COLS, COLS) * weight, axis=0, keepdims=True)
            out = jnp.where(sub == k, line, out)
        ends_at = mixed(K * COLS, 2 * K)
        out = out + ends_at[:K] * jnp.where(next_col == -1, size_y, 0.0)
        out = out + ends_at[K:] * jnp.where(next_col == COLS, size_y, 0.0)
        scaled_ref[:, pl.ds(at, CHUNK)] = out / jnp.sqrt(err_ref[:, pl.ds(at, CHUNK)])
        return carry

    lax.fori_loop(0, OBS // CHUNK, sample, 0)

    scaled = scaled_ref[...]
    normal = lax.dot_general(
        scaled, scaled, contract_last, precision=highest, preferred_element_type=F32
    )
    row = gram_row
    wide = jnp.concatenate([normal, jnp.zeros((K, COLS - K), F32)], axis=1)
    for i in range(K):
        row = row + roll(wide[i : i + 1], K * K + K * i, 1)
    sums_ref[...] = row


def inverse_of_factor(a):
    n = len(a)
    low = [[None] * n for _ in range(n)]
    inv = [[None] * n for _ in range(n)]
    for j in range(n):
        total = a[j][j]
        for k in range(j):
            total = total - low[j][k] * low[j][k]
        root = jnp.sqrt(total)
        inv[j][j] = 1.0 / root
        for i in range(j + 1, n):
            total = a[i][j]
            for k in range(j):
                total = total - low[i][k] * low[j][k]
            low[i][j] = total * inv[j][j]
    for j in range(n):
        for i in range(j + 1, n):
            total = low[i][j] * inv[j][j]
            for k in range(j + 1, i):
                total = total + low[i][k] * inv[k][j]
            inv[i][j] = -total * inv[i][i]
    return inv


def added(terms):
    total = terms[0]
    for term in terms[1:]:
        total = total + term
    return total


def final_kernel(cells_all, obs_all, sums_ref, bred_ref, scaled_ref, analysis_ref, perturb_ref):
    row = sums_ref[...]
    tile = (ROWS, COLS)

    def entry(at):
        return jnp.broadcast_to(row[:, at : at + 1], tile)

    gram = [[entry(i * K + j) / cells_all if j <= i else None for j in range(K)] for i in range(K)]
    normal = [[None] * K for _ in range(K)]
    for i in range(K):
        for j in range(i + 1):
            normal[i][j] = normal[j][i] = entry(K * K + i * K + j) / obs_all
    inv_lower = inverse_of_factor(gram)
    half = [
        [added([inv_lower[i][k] * normal[k][j] for k in range(i + 1)]) for j in range(K)]
        for i in range(K)
    ]
    system = [
        [
            added([half[i][k] * inv_lower[j][k] for k in range(j + 1)]) + (1.0 if i == j else 0.0)
            for j in range(i + 1)
        ]
        for i in range(K)
    ]
    inv_factor = inverse_of_factor(system)
    combo = [
        [added([inv_factor[i][k] * inv_lower[k][j] for k in range(j, i + 1)]) for j in range(i + 1)]
        for i in range(K)
    ]
    for plane in range(PLANES):
        fields = [bred_ref[j * PLANES + plane] for j in range(K)]
        for k in range(K):
            analysis_ref[k * PLANES + plane] = added(
                [combo[k][j] * fields[j] for j in range(k + 1)]
            )
    sub = iota(tile, 0)
    columns = []
    for j in range(K):
        column = jnp.zeros(tile, F32)
        for k in range(j, K):
            column = jnp.where(sub == k, combo[k][j], column)
        columns.append(column)
    for at in range(0, OBS, COLS):
        part = scaled_ref[:, at : at + COLS]
        perturb_ref[:, at : at + COLS] = added(
            [columns[j] * part[j : j + 1] for j in range(K)]
        )


def shape(*dims):
    return jax.ShapeDtypeStruct(dims, F32)


def swap(packed, axes):
    count = lax.axis_size(axes)
    first = [(i, i ^ 1) for i in range(count)]
    second = [((i - 1) % count, ((i ^ 1) - 1) % count) for i in range(count)]
    return lax.ppermute(packed[0], axes, first), lax.ppermute(packed[1], axes, second)


def small(mib):
    return pltpu.CompilerParams(vmem_limit_bytes=mib << 20)


def spread(row, axes):
    count = lax.axis_size(axes)
    copies = jnp.broadcast_to(row[None], (count, 1, COLS))
    return lax.all_to_all(copies, axes, 0, 0, tiled=True).sum(axis=0)


def local(vectors, background, obs_site, obs_offset, obs_error):
    devices_all = lax.axis_size(GX) * lax.axis_size(GY)
    cells_all = float(PLANES * ROWS * COLS * devices_all)
    obs_all = float(OBS * devices_all)
    vec = vectors.reshape(K * PLANES, ROWS, COLS)
    back = background.reshape(PLANES, ROWS, COLS)
    packed = pl.pallas_call(
        pack_rows_kernel,
        out_shape=(shape(HALF, ROWS, COLS),) * 2,
        scratch_shapes=[pltpu.VMEM((FIELDS, ROWS, COLS), F32)],
        compiler_params=small(8),
        name="pack_rows",
    )(vec, back)
    got = swap(packed, GX)
    ext, *packed = pl.pallas_call(
        pack_cols_kernel,
        out_shape=(shape(FIELDS, 2 * ROWS, COLS),) + (shape(GROUPS, 2 * ROWS, COLS),) * 2,
        compiler_params=small(8),
        name="pack_cols",
    )(vec, back, *got)
    got = swap(packed, GY)
    bred, scaled, sums = pl.pallas_call(
        main_kernel,
        out_shape=(shape(K * PLANES, ROWS, COLS), shape(K, OBS), shape(1, COLS)),
        scratch_shapes=[
            pltpu.VMEM((FIELDS, 2 * ROWS, COLS), F32),
            pltpu.VMEM((K, COLS, COLS), F32),
            pltpu.VMEM((K, COLS, COLS), F32),
            pltpu.VMEM((K * COLS + 2 * K, 2 * COLS), jnp.bfloat16),
            pltpu.VMEM((COLS, COLS), F32),
        ],
        compiler_params=small(16),
        name="advance_sample",
    )(ext, *got, obs_site.reshape(1, OBS), obs_offset, obs_error.reshape(1, OBS))
    sums = spread(spread(sums, FLAT), DEEP)
    analysis, perturb = pl.pallas_call(
        functools.partial(final_kernel, cells_all, obs_all),
        out_shape=(shape(K * PLANES, ROWS, COLS), shape(K, OBS)),
        compiler_params=small(8),
        name="combine",
    )(sums, bred, scaled)
    return (analysis.reshape(vectors.shape), perturb)


def solution(mesh):
    torus = Mesh(mesh.devices.reshape(8, 4, 2, 4, 2), GX_GY)
    return jax.shard_map(
        local,
        mesh=torus,
        in_specs=(
            P(None, None, None, GX, GY),
            P(None, None, GX, GY),
            P(GX_GY),
            P(None, GX_GY),
            P(GX_GY),
        ),
        out_specs=(P(None, None, None, GX, GY), P(None, GX_GY)),
        check_vma=False,
    )
```

time: 243 us -> 97.8 us (0.40)
  local copies, waits for them, and re-layouts: 100 us -> 1.83 us
  blocking collectives: 82.7 us -> 45.1 us
  other arithmetic: 20.5 us -> 0.04 us
  Pallas kernels: 0 us -> 17.3 us
  matrix products: 3.89 us -> 0 us
    psum x5 -> x0, blocking collectives: 82.7 us -> none  [over_axes(): value = lax.psum(value, axis)]
    all_to_all x0 -> x2, blocking collectives: none -> 45.1 us  [spread(): return lax.all_to_all(copies, axes, 0, 0, tiled=True).sum(axis=0)]
    reshape x9 -> x0, local copies, waits for them, and re-layouts: 37.9 us -> none  [the longest x8 33.9 us: sample(): windows.append(window.reshape(vector_count, -1))]
    concatenate x1 -> x0, local copies, waits for them, and re-layouts: 34.1 us -> none  [sample(): table = jnp.concatenate(windows, axis=0).T]
    pallas_call x0 -> x4, Pallas kernels: none -> 17.3 us  [the longest x1 15.6 us: local(): pl.pallas_call(main_kernel, out_shape=(shape(K * PLANES, ROWS, COLS), sha...]
    gather x2 -> x0, local copies, waits for them, and re-layouts: 15.2 us -> none  [sample(): jnp.take(table, obs_site, axis=0)]
    another operation x16 -> x0, other arithmetic: 11 us -> none  [the longest x6 5.62 us: tendency(): return jnp.stack([tend_east, tend_north, tend_height], axis=1)]
    slice x4 -> x0, local copies, waits for them, and re-layouts: 4.51 us -> none  [the longest x2 2.01 us: padded_2(): lax.slice_in_dim(block, block.shape[dim] - width, None, axis=dim)]
  transfers between devices with their start and end apart: 4 -> 4, of which waited for: 3 -> 2; matrix products, arithmetic and copies ran while one was open for 2% -> 0% of each run, Pallas kernels for 0% -> 0%
where the time goes in v1:
time: 97.8 us; the launch traced here: 97.3 us
  blocking collectives  45.1 us (46%)
  starting transfers between devices  26 us (27%)
  Pallas kernels  17.3 us (18%)
  waiting for transfers between devices  6.41 us (7%)
  local copies, waits for them, and re-layouts  1.83 us (2%)
    all_to_all x2, blocking collectives, spread(): return lax.all_to_all(copies, axes, 0, 0, tiled=True).sum(axis=0)  45.1 us
    ppermute x2, starting transfers between devices, swap(): lax.ppermute(packed[1], axes, second)  17.1 us
    pallas_call x1, Pallas kernels, local(): pl.pallas_call(main_kernel, out_shape=(shape(K * PLANES, ROWS, COLS), sha...  15.6 us
    ppermute x2, starting transfers between devices, swap(): lax.ppermute(packed[0], axes, first)  8.89 us
    ppermute x2, waiting for transfers between devices, swap(): lax.ppermute(packed[1], axes, second)  6.4 us
  transfers between devices with their start and end apart: 4, of which 2 were waited for; matrix products, arithmetic and copies ran while one was open for 0% of the time, Pallas kernels for 0%

profile of v1, /device:TPU:1, one launch (start us, length us, event | category | flops | bytes accessed | tf_op | source)
XLA Modules:
  0.0 97.3 jit_solution(8831293197376536600)
XLA Ops:
  0.6 0.0 copy-start
  0.6 1.0 %copy-done = f32[8,3,4,8,128]{4,3,2,1,0:T(8,128)S(1)} copy-done((f32[8,3,4,8,128]{4,3,2,1,0:T(8,128)S(1)}, f32[8,3,4,8,128]{4,3,2,1,0:T(8,128)}, u32[]{:S(2)}) %copy-start) | copy-done | bytes 393240
  1.6 0.0 copy-start.1
  1.6 0.8 copy-done.1
  2.4 0.1 pack_rows.1
  2.5 4.0 %collective-permute-start = (f32[54,8,128]{2,1,0:T(8,128)S(1)}, f32[54,8,128]{2,1,0:T(8,128)S(1)}, u32[]{:S(2)}, u32[]{:S(2)}) collective-permute-start(f32[54,8,128]{2,1,0:T(8,128)S(1)} %get-tuple-element.12), channel_id=1, source_target_pairs={{0,16},{16,0},{32,48},{48,32},{64,80},{80,64},{96,112},{112,96},{1... | collective-permute-start | bytes 663560 | tf_op jit(solution)/shard_map/ppermute | solution.py:347
  6.5 0.0 copy-start.2
  6.5 14.5 %collective-permute-start.1 = (f32[54,8,128]{2,1,0:T(8,128)S(1)}, f32[54,8,128]{2,1,0:T(8,128)S(1)}, u32[]{:S(2)}, u32[]{:S(2)}) collective-permute-start(f32[54,8,128]{2,1,0:T(8,128)S(1)} %get-tuple-element.13), channel_id=1, source_target_pairs={{496,0},{0,496},{16,32},{32,16},{48,64},{64,48},{80,96},{96,80},{1... | collective-permute-start | bytes 663560 | tf_op jit(solution)/shard_map/ppermute | solution.py:347
  21.0 0.0 collective-permute-done.got_one
  21.0 3.8 %collective-permute-done.1.got_two = f32[54,8,128]{2,1,0:T(8,128)S(1)} collective-permute-done((f32[54,8,128]{2,1,0:T(8,128)S(1)}, f32[54,8,128]{2,1,0:T(8,128)S(1)}, u32[]{:S(2)}, u32[]{:S(2)}) %collective-permute-start.1) | collective-permute-done | bytes 221216 | tf_op jit(solution)/shard_map/ppermute | solution.py:347
  24.8 0.0 copy-start.3
  24.8 0.0 copy-start.4
  24.8 0.3 pack_cols.1
  25.2 4.9 %collective-permute-start.2 = (f32[4,16,128]{2,1,0:T(8,128)S(1)}, f32[4,16,128]{2,1,0:T(8,128)S(1)}, u32[]{:S(2)}, u32[]{:S(2)}) collective-permute-start(f32[4,16,128]{2,1,0:T(8,128)S(1)} %get-tuple-element.15), channel_id=1, source_target_pairs={{0,1},{1,0},{2,3},{3,2},{4,5},{5,4},{6,7},{7,6},{8,9},{9,8},{10,11... | collective-permute-start | bytes 98312 | tf_op jit(solution)/shard_map/ppermute | solution.py:347
  30.0 2.6 %collective-permute-start.3 = (f32[4,16,128]{2,1,0:T(8,128)S(1)}, f32[4,16,128]{2,1,0:T(8,128)S(1)}, u32[]{:S(2)}, u32[]{:S(2)}) collective-permute-start(f32[4,16,128]{2,1,0:T(8,128)S(1)} %get-tuple-element.16), channel_id=1, source_target_pairs={{15,0},{0,15},{1,2},{2,1},{3,4},{4,3},{5,6},{6,5},{7,8},{8,7},{9,1... | collective-permute-start | bytes 98312 | tf_op jit(solution)/shard_map/ppermute | solution.py:347
  32.6 0.0 collective-permute-done.2.got_one
  32.7 2.6 %collective-permute-done.3.got_two = f32[4,16,128]{2,1,0:T(8,128)S(1)} collective-permute-done((f32[4,16,128]{2,1,0:T(8,128)S(1)}, f32[4,16,128]{2,1,0:T(8,128)S(1)}, u32[]{:S(2)}, u32[]{:S(2)}) %collective-permute-start.3) | collective-permute-done | bytes 32800 | tf_op jit(solution)/shard_map/ppermute | solution.py:347
  35.3 0.0 copy-done.2
  35.3 0.0 copy-done.3
  35.3 0.0 copy-done.4
  35.3 15.6 %advance_sample.1 = (f32[96,8,128]{2,1,0:T(8,128)S(1)}, f32[8,4096]{1,0:T(8,128)S(1)}, f32[1,128]{1,0:T(1,128)S(1)}) custom-call(f32[108,16,128]{2,1,0:T(8,128)S(1)} %get-tuple-element.14.ext_ref, f32[4,16,128]{2,1,0:T(8,128)S(1)} %collective-permute-done.2.got_one, f32[4,16,128]{2,1,0:T(8,128)S(1)} %collective-permute-done.3.got_two, ...), custom_call_target="tpu_custom_call" | custom-call | tf_op jit(solution)/shard_map/advance_sample/pallas_call | solution.py:381
  50.9 21.5 %all_to_all.10 = f32[32,1,128]{2,1,0:T(1,128)S(1)} all-to-all(f32[32,1,128]{2,1,0:T(1,128)S(1)} %broadcast_in_dim.7), channel_id=1, replica_groups=mesh['z_lo'=8,'y'=4,'z_hi'=2,'x'=4,'core'=2] {'y','x','core'}, dimensions={0} | all-to-all | bytes 32768 | tf_op jit(solution)/shard_map/all_to_all | solution.py:357
  72.4 23.6 %all_to_all.11 = f32[16,1,128]{2,1,0:T(1,128)S(1)} all-to-all(f32[16,1,128]{2,1,0:T(1,128)S(1)} %broadcast_in_dim.16), channel_id=1, replica_groups=mesh['z_lo'=8,'y'=4,'z_hi'=2,'x'=4,'core'=2] {'z_lo','z_hi'}, dimensions={0} | all-to-all | bytes 16384 | tf_op jit(solution)/shard_map/all_to_all | solution.py:357
  96.0 1.3 %combine.1 = (f32[96,8,128]{2,1,0:T(8,128)}, f32[8,4096]{1,0:T(8,128)}) custom-call(f32[1,128]{1,0:T(1,128)S(1)} %bitcast.15, f32[96,8,128]{2,1,0:T(8,128)S(1)} %get-tuple-element.18.bred_ref, f32[8,4096]{1,0:T(8,128)S(1)} %get-tuple-element.19.scaled_ref), custom_call_target="tpu_custom_call" | custom-call | tf_op jit(solution)/shard_map/combine/pallas_call | solution.py:395
  (4 shorter events, 0.1 us)
Async XLA Ops:
  0.6 1.0 %copy-start = (f32[8,3,4,8,128]{4,3,2,1,0:T(8,128)S(1)}, f32[8,3,4,8,128]{4,3,2,1,0:T(8,128)}, u32[]{:S(2)}) copy-start(f32[8,3,4,8,128]{4,3,2,1,0:T(8,128)} %param.5) | copy-start | bytes 1179652
  1.6 0.8 copy-start.1
  2.5 18.5 %collective-permute-start = (f32[54,8,128]{2,1,0:T(8,128)S(1)}, f32[54,8,128]{2,1,0:T(8,128)S(1)}, u32[]{:S(2)}, u32[]{:S(2)}) collective-permute-start(f32[54,8,128]{2,1,0:T(8,128)S(1)} %get-tuple-element.12), channel_id=1, source_target_pairs={{0,16},{16,0},{32,48},{48,32},{64,80},{80,64},{96,112},{112,96},{1... | collective-permute-start | bytes 663560 | tf_op jit(solution)/shard_map/ppermute | solution.py:347
  6.5 28.7 %copy-start.2 = (f32[2,4096]{1,0:T(2,128)S(1)}, f32[2,4096]{1,0:T(2,128)}, u32[]{:S(2)}) copy-start(f32[2,4096]{1,0:T(2,128)} %off_ref.1) | copy-start | bytes 98308
  6.5 18.3 %collective-permute-start.1 = (f32[54,8,128]{2,1,0:T(8,128)S(1)}, f32[54,8,128]{2,1,0:T(8,128)S(1)}, u32[]{:S(2)}, u32[]{:S(2)}) collective-permute-start(f32[54,8,128]{2,1,0:T(8,128)S(1)} %get-tuple-element.13), channel_id=1, source_target_pairs={{496,0},{0,496},{16,32},{32,16},{48,64},{64,48},{80,96},{96,80},{1... | collective-permute-start | bytes 663560 | tf_op jit(solution)/shard_map/ppermute | solution.py:347
  24.8 10.4 %copy-start.3 = (s32[4096]{0:T(1024)S(1)}, s32[4096]{0:T(1024)}, u32[]{:S(2)}) copy-start(s32[4096]{0:T(1024)} %param.7) | copy-start | bytes 49156
  24.8 10.4 %copy-start.4 = (f32[4096]{0:T(1024)S(1)}, f32[4096]{0:T(1024)}, u32[]{:S(2)}) copy-start(f32[4096]{0:T(1024)} %param.9) | copy-start | bytes 49156
  25.2 7.5 %collective-permute-start.2 = (f32[4,16,128]{2,1,0:T(8,128)S(1)}, f32[4,16,128]{2,1,0:T(8,128)S(1)}, u32[]{:S(2)}, u32[]{:S(2)}) collective-permute-start(f32[4,16,128]{2,1,0:T(8,128)S(1)} %get-tuple-element.15), channel_id=1, source_target_pairs={{0,1},{1,0},{2,3},{3,2},{4,5},{5,4},{6,7},{7,6},{8,9},{9,8},{10,11... | collective-permute-start | bytes 98312 | tf_op jit(solution)/shard_map/ppermute | solution.py:347
  30.0 5.2 %collective-permute-start.3 = (f32[4,16,128]{2,1,0:T(8,128)S(1)}, f32[4,16,128]{2,1,0:T(8,128)S(1)}, u32[]{:S(2)}, u32[]{:S(2)}) collective-permute-start(f32[4,16,128]{2,1,0:T(8,128)S(1)} %get-tuple-element.16), channel_id=1, source_target_pairs={{15,0},{0,15},{1,2},{2,1},{3,4},{4,3},{5,6},{6,5},{7,8},{8,7},{9,1... | collective-permute-start | bytes 98312 | tf_op jit(solution)/shard_map/ppermute | solution.py:347

commit v2 on v1

--- a/solution.py
+++ b/solution.py
@@ -22,9 +22,10 @@
 FIELDS = K * PLANES + PLANES
 HALF = FIELDS // 2
 GROUPS = 4
-PER_GROUP = FIELDS // GROUPS
-CHUNK = 256
-BATCH = 2
+STRIPS = 2 * PLANES + L
+CHUNK = 512
+BATCH = 4
+OWN = PLANES * ROWS
 STEP = 0.35
 F32 = jnp.float32
 highest = lax.Precision.HIGHEST
@@ -61,7 +62,7 @@
     two_ref[...] = jnp.where(odd, up, down)
 
 
-def pack_cols_kernel(vec_ref, back_ref, got_one, got_two, ext_ref, one_ref, two_ref):
+def pack_cols_kernel(vec_ref, back_ref, got_one, got_two, ext_ref, strip_ref, one_ref, two_ref):
     at_odd_row = odd_row()
     at_odd_col = odd_col()
     ext_ref[0 : K * PLANES, 0:ROWS] = vec_ref[...]
@@ -72,15 +73,33 @@
     ext_ref[0:HALF, ROWS : 2 * ROWS] = jnp.where(top, high, low)
     ext_ref[HALF:FIELDS, ROWS : 2 * ROWS] = roll(jnp.where(top, low, high), 4, 1)
     lane = iota((2 * ROWS, COLS), 1)
+    eighth = lax.rem(lane, 32) // 4
     for group in range(GROUPS):
         up = jnp.zeros((2 * ROWS, COLS), F32)
         down = jnp.zeros((2 * ROWS, COLS), F32)
-        for m in range(PER_GROUP):
-            moved = roll(ext_ref[group * PER_GROUP + m], 4 * m, 1)
-            down = jnp.where(lane // 4 == m, moved, down)
-            up = jnp.where(lane // 4 == (m + 31) % 32, moved, up)
+        for u in range(8):
+            t = group * 8 + u
+            if t >= STRIPS:
+                break
+            strip = jnp.zeros((2 * ROWS, COLS), F32)
+            for kk, field in enumerate(strip_fields(t)):
+                plane = ext_ref[field]
+                left = (lane >= 32 * kk + 4) & (lane < 32 * kk + 16)
+                right = (lane >= 32 * kk + 16) & (lane < 32 * kk + 28)
+                strip = jnp.where(left, roll(plane, 32 * kk + 4, 1), strip)
+                strip = jnp.where(right, roll(plane, 32 * kk + 28, 1), strip)
+            strip_ref[t] = strip
+            down = jnp.where(eighth == u, roll(strip, 4 * u - 4, 1), down)
+            up = jnp.where(eighth == u, roll(strip, 4 * u - 24, 1), up)
         one_ref[group] = jnp.where(at_odd_col, down, up)
         two_ref[group] = jnp.where(at_odd_col, up, down)
+
+
+def strip_fields(t):
+    if t < 2 * PLANES:
+        plane, half = t // 2, t % 2
+        return [(half * 4 + kk) * PLANES + plane for kk in range(4)]
+    return [K * PLANES + c * L + t - 2 * PLANES for c in range(3)]
 
 
 def tendency(state, back):
@@ -111,55 +130,132 @@
     ]
 
 
+def put_rows(ref, k, plane, field):
+    ref[k, plane * ROWS : (plane + 1) * ROWS] = field[:ROWS]
+    ref[k, OWN + plane : OWN + plane + 1] = field[2 * ROWS - 1 :]
+    ref[k, OWN + PLANES + plane : OWN + PLANES + plane + 1] = field[ROWS : ROWS + 1]
+
+
+def advance_kernel(ext_ref, rows_ref):
+    rows_ref[:, OWN + 2 * PLANES :] = jnp.zeros((K, COLS - OWN - 2 * PLANES, COLS), F32)
+    for level in range(L):
+        base = K * PLANES + level
+        back = [ext_ref[base + c * L][None] for c in range(3)]
+
+        def body(i, carry, level=level, back=back):
+            start = [
+                jnp.stack(
+                    [ext_ref[(i * BATCH + b) * PLANES + c * L + level] for b in range(BATCH)]
+                )
+                for c in range(3)
+            ]
+            done = advance(start, back)
+            for c in range(3):
+                for b in range(BATCH):
+                    put_rows(rows_ref, i * BATCH + b, c * L + level, done[c][b])
+            return carry
+
+        lax.fori_loop(0, K // BATCH, body, 0)
+
+
+def weights_kernel(site_ref, off_ref, err_ref, pick_ref, weight_ref, ends_ref):
+    def step(i, carry):
+        at = pl.ds(pl.multiple_of(i * CHUNK, CHUNK), CHUNK)
+        site = site_ref[:, at]
+        shift_x = off_ref[0:1, at]
+        shift_y = off_ref[1:2, at]
+        row_at = site // COLS
+        plane = site // (ROWS * COLS)
+        row = row_at % ROWS
+        col = site % COLS
+        size_x = jnp.abs(shift_x)
+        size_y = jnp.abs(shift_y)
+        before = jnp.where(row == 0, OWN + plane, row_at - 1)
+        after = jnp.where(row == ROWS - 1, OWN + PLANES + plane, row_at + 1)
+        beside = jnp.where(shift_x < 0.0, before, after)
+        next_col = jnp.where(shift_y < 0.0, col - 1, col + 1)
+        own_x = 1.0 - size_x
+        scale = 1.0 / jnp.sqrt(err_ref[:, at])
+        own_y = (1.0 - size_y) * scale
+        side_y = size_y * scale
+
+        def split(value):
+            high = value.astype(jnp.bfloat16).astype(F32)
+            return high, value - high
+
+        own_high, own_low = split(own_x)
+        side_high, side_low = split(size_x)
+        index = iota((COLS, CHUNK), 0)
+        at_own = index == row_at
+        at_side = index == beside
+        pick_high = jnp.where(at_own, own_high, jnp.where(at_side, side_high, 0.0))
+        pick_low = jnp.where(at_own, own_low, jnp.where(at_side, side_low, 0.0))
+        pick_ref[0:COLS, at] = pick_high.astype(jnp.bfloat16)
+        pick_ref[COLS : 2 * COLS, at] = pick_low.astype(jnp.bfloat16)
+        weight_ref[:, at] = jnp.where(
+            index == col, own_y, jnp.where(index == next_col, side_y, 0.0)
+        )
+        ends_ref[0:1, at] = jnp.where(next_col == -1, side_y, 0.0)
+        ends_ref[1:2, at] = jnp.where(next_col == COLS, side_y, 0.0)
+        return carry
+
+    lax.fori_loop(0, OBS // CHUNK, step, 0)
+
+
 def main_kernel(
-    ext_ref, got_one, got_two, site_ref, off_ref, err_ref,
+    rows_ref, strip_ref, got_one, got_two, pick_ref, weight_ref, ends_ref,
     bred_ref, scaled_ref, sums_ref,
-    side_ref, rows_ref, edge_ref, table_ref, pair_ref,
+    whole_ref, side_ref, table_ref, pair_ref,
 ):
     at_odd_col = odd_col()
     lane = iota((2 * ROWS, COLS), 1)
+    eighth = lax.rem(lane, 32) // 4
     for group in range(GROUPS):
         left = jnp.where(at_odd_col, got_one[group], got_two[group])
         right = jnp.where(at_odd_col, got_two[group], got_one[group])
-        for m in range(PER_GROUP):
-            moved = jnp.where(lane < 4, roll(right, -4 * m, 1), roll(left, -4 * m, 1))
-            moved = jnp.where((lane < 4) | (lane >= COLS - 4), moved, 0.0)
-            side_ref[group * PER_GROUP + m] = moved
-
-    rows_ref[:, PLANES * ROWS + 2 * PLANES :, :] = jnp.zeros((K, COLS - 10 * PLANES, COLS), F32)
-    edge_ref[:, PLANES * ROWS + 2 * PLANES :, :] = jnp.zeros((K, COLS - 10 * PLANES, COLS), F32)
+        for u in range(8):
+            t = group * 8 + u
+            if t >= STRIPS:
+                break
+            strip = jnp.where(eighth == 0, roll(left, -4 * u, 1), strip_ref[t])
+            whole_ref[t] = jnp.where(eighth == 7, roll(right, 28 - 4 * u, 1), strip)
+    side_ref[:, OWN + 2 * PLANES :] = jnp.zeros((2, COLS - OWN - 2 * PLANES, COLS), F32)
     for level in range(L):
-        base = K * PLANES + level
-        back = [
-            jnp.concatenate([ext_ref[base + c * L], side_ref[base + c * L]], axis=-1)[None]
-            for c in range(3)
+        mixed_back = whole_ref[2 * PLANES + level]
+        back = []
+        for c in range(3):
+            spread_back = mixed_back
+            for kk in range(4):
+                if kk != c:
+                    spread_back = jnp.where(
+                        lane // 32 == kk, roll(mixed_back, 32 * (kk - c), 1), spread_back
+                    )
+            back.append(spread_back[None])
+        start = [
+            whole_ref[2 * (c * L + level) : 2 * (c * L + level) + 2] for c in range(3)
         ]
-
-        def body(i, carry, level=level, back=back):
-            start = []
-            for c in range(3):
-                parts = []
-                for b in range(BATCH):
-                    at = (i * BATCH + b) * PLANES + c * L + level
-                    parts.append(jnp.concatenate([ext_ref[at], side_ref[at]], axis=-1)[None])
-                start.append(jnp.concatenate(parts, axis=0))
-            done = advance(start, back)
-            for c in range(3):
-                plane = c * L + level
-                for b in range(BATCH):
-                    k = i * BATCH + b
-                    field = done[c][b]
-                    main, side = field[:, :COLS], field[:, COLS:]
-                    bred_ref[k * PLANES + plane] = main[:ROWS]
-                    for ref, part in ((rows_ref, main), (edge_ref, side)):
-                        ref[k, plane * ROWS : (plane + 1) * ROWS] = part[:ROWS]
-                        at = PLANES * ROWS + plane
-                        ref[k, at : at + 1] = part[2 * ROWS - 1 :]
-                        at = PLANES * ROWS + PLANES + plane
-                        ref[k, at : at + 1] = part[ROWS : ROWS + 1]
-            return carry
-
-        lax.fori_loop(0, K // BATCH, body, 0)
+        done = advance(start, back)
+        for c in range(3):
+            for half in range(2):
+                put_rows(side_ref, half, c * L + level, done[c][half])
+
+    def put(at, count, value):
+        high = value.astype(jnp.bfloat16)
+        low = (value - high.astype(F32)).astype(jnp.bfloat16)
+        table_ref[at : at + count, 0:COLS] = high
+        table_ref[at : at + count, COLS : 2 * COLS] = low
+
+    lane = iota((COLS, COLS), 1)
+    for k in range(K):
+        side, kk = side_ref[k // 4], k % 4
+        fields = jnp.where(lane < 3, roll(side, -(32 * kk + 4), 1), rows_ref[k])
+        fields = jnp.where(lane >= COLS - 3, roll(side, 100 - 32 * kk, 1), fields)
+        bred_ref[k * PLANES : (k + 1) * PLANES] = fields[:OWN].reshape(PLANES, ROWS, COLS)
+        put(k * COLS, COLS, fields.T)
+    across = [side_ref[half].T for half in range(2)]
+    lines = [across[k // 4][32 * (k % 4) + 3 :][:1] for k in range(K)]
+    lines += [across[k // 4][32 * (k % 4) + 28 :][:1] for k in range(K)]
+    put(K * COLS, 2 * K, jnp.concatenate(lines, axis=0))
 
     for i in range(K):
         mine = bred_ref[i * PLANES : (i + 1) * PLANES]
@@ -176,55 +272,12 @@
         precision=highest, preferred_element_type=F32,
     )[0:1]
 
-    def put(at, count, value):
-        high = value.astype(jnp.bfloat16)
-        low = (value - high.astype(F32)).astype(jnp.bfloat16)
-        table_ref[at : at + count, 0:COLS] = high
-        table_ref[at : at + count, COLS : 2 * COLS] = low
-
-    ends = jnp.zeros((COLS, COLS), F32)
-    lane = iota((COLS, COLS), 1)
-    for k in range(K):
-        put(k * COLS, COLS, rows_ref[k].T)
-        edge = edge_ref[k]
-        ends = jnp.where(lane == k, roll(edge, k + 1, 1), ends)
-        ends = jnp.where(lane == K + k, roll(edge, K + k, 1), ends)
-    put(K * COLS, 2 * K, ends.T[: 2 * K])
-
     def sample(step, carry):
-        at = pl.multiple_of(step * CHUNK, CHUNK)
-        site = site_ref[:, pl.ds(at, CHUNK)]
-        shift_x = off_ref[0:1, pl.ds(at, CHUNK)]
-        shift_y = off_ref[1:2, pl.ds(at, CHUNK)]
-        row_at = site // COLS
-        plane = site // (ROWS * COLS)
-        row = row_at % ROWS
-        col = site % COLS
-        size_x = jnp.abs(shift_x)
-        size_y = jnp.abs(shift_y)
-        before = jnp.where(row == 0, PLANES * ROWS + plane, row_at - 1)
-        after = jnp.where(row == ROWS - 1, PLANES * ROWS + PLANES + plane, row_at + 1)
-        beside = jnp.where(shift_x < 0.0, before, after)
-        next_col = jnp.where(shift_y < 0.0, col - 1, col + 1)
-        own_x = 1.0 - size_x
-        own_y = 1.0 - size_y
-
-        def split(value):
-            high = value.astype(jnp.bfloat16).astype(F32)
-            return high, value - high
-
-        own_high, own_low = split(own_x)
-        side_high, side_low = split(size_x)
-        index = iota((COLS, CHUNK), 0)
-        at_own = index == row_at
-        at_side = index == beside
-        pick_high = jnp.where(at_own, own_high, jnp.where(at_side, side_high, 0.0))
-        pick_low = jnp.where(at_own, own_low, jnp.where(at_side, side_low, 0.0))
-        pick_high = pick_high.astype(jnp.bfloat16)
-        pick_low = pick_low.astype(jnp.bfloat16)
-        weight = jnp.where(index == col, own_y, jnp.where(index == next_col, size_y, 0.0))
-        high2 = jnp.concatenate([pick_high, pick_high], axis=0)
-        low2 = jnp.concatenate([pick_low, pick_low], axis=0)
+        at = pl.ds(pl.multiple_of(step * CHUNK, CHUNK), CHUNK)
+        high, low = pick_ref[0:COLS, at], pick_ref[COLS : 2 * COLS, at]
+        high2 = jnp.concatenate([high, high], axis=0)
+        low2 = jnp.concatenate([low, low], axis=0)
+        weight = weight_ref[:, at]
 
         def mixed(start, count):
             part = table_ref[start : start + count]
@@ -238,9 +291,9 @@
             line = jnp.sum(mixed(k * COLS, COLS) * weight, axis=0, keepdims=True)
             out = jnp.where(sub == k, line, out)
         ends_at = mixed(K * COLS, 2 * K)
-        out = out + ends_at[:K] * jnp.where(next_col == -1, size_y, 0.0)
-        out = out + ends_at[K:] * jnp.where(next_col == COLS, size_y, 0.0)
-        scaled_ref[:, pl.ds(at, CHUNK)] = out / jnp.sqrt(err_ref[:, pl.ds(at, CHUNK)])
+        out = out + ends_at[:K] * ends_ref[0:1, at]
+        out = out + ends_at[K:] * ends_ref[1:2, at]
+        scaled_ref[:, at] = out
         return carry
 
     lax.fori_loop(0, OBS // CHUNK, sample, 0)
@@ -344,7 +397,8 @@
     count = lax.axis_size(axes)
     first = [(i, i ^ 1) for i in range(count)]
     second = [((i - 1) % count, ((i ^ 1) - 1) % count) for i in range(count)]
-    return lax.ppermute(packed[0], axes, first), lax.ppermute(packed[1], axes, second)
+    other = lax.ppermute(packed[1], axes, second)
+    return lax.ppermute(packed[0], axes, first), other
 
 
 def small(mib):
@@ -355,6 +409,25 @@
     count = lax.axis_size(axes)
     copies = jnp.broadcast_to(row[None], (count, 1, COLS))
     return lax.all_to_all(copies, axes, 0, 0, tiled=True).sum(axis=0)
+
+
+def main_call(*operands):
+    return pl.pallas_call(
+        main_kernel,
+        out_shape=(shape(K * PLANES, ROWS, COLS), shape(K, OBS), shape(1, COLS)),
+        scratch_shapes=[
+            pltpu.VMEM((STRIPS, 2 * ROWS, COLS), F32),
+            pltpu.VMEM((2, COLS, COLS), F32),
+            pltpu.VMEM((K * COLS + 2 * K, 2 * COLS), jnp.bfloat16),
+            pltpu.VMEM((COLS, COLS), F32),
+        ],
+        compiler_params=small(16),
+        name="advance_sample",
+    )(*operands)
+
+
+def busy(us):
+    return pl.CostEstimate(flops=us * 10**9, bytes_accessed=0, transcendentals=0)
 
 
 def local(vectors, background, obs_site, obs_offset, obs_error):
@@ -371,26 +444,31 @@
         name="pack_rows",
     )(vec, back)
     got = swap(packed, GX)
-    ext, *packed = pl.pallas_call(
+    weights = pl.pallas_call(
+        weights_kernel,
+        out_shape=(
+            jax.ShapeDtypeStruct((2 * COLS, OBS), jnp.bfloat16), shape(COLS, OBS), shape(2, OBS)
+        ),
+        compiler_params=small(8),
+        cost_estimate=busy(3),
+        name="weights",
+    )(obs_site.reshape(1, OBS), obs_offset, obs_error.reshape(1, OBS))
+    ext, strips, *packed = pl.pallas_call(
         pack_cols_kernel,
-        out_shape=(shape(FIELDS, 2 * ROWS, COLS),) + (shape(GROUPS, 2 * ROWS, COLS),) * 2,
+        out_shape=(shape(FIELDS, 2 * ROWS, COLS), shape(STRIPS, 2 * ROWS, COLS))
+        + (shape(GROUPS, 2 * ROWS, COLS),) * 2,
         compiler_params=small(8),
         name="pack_cols",
     )(vec, back, *got)
     got = swap(packed, GY)
-    bred, scaled, sums = pl.pallas_call(
-        main_kernel,
-        out_shape=(shape(K * PLANES, ROWS, COLS), shape(K, OBS), shape(1, COLS)),
-        scratch_shapes=[
-            pltpu.VMEM((FIELDS, 2 * ROWS, COLS), F32),
-            pltpu.VMEM((K, COLS, COLS), F32),
-            pltpu.VMEM((K, COLS, COLS), F32),
-            pltpu.VMEM((K * COLS + 2 * K, 2 * COLS), jnp.bfloat16),
-            pltpu.VMEM((COLS, COLS), F32),
-        ],
-        compiler_params=small(16),
-        name="advance_sample",
-    )(ext, *got, obs_site.reshape(1, OBS), obs_offset, obs_error.reshape(1, OBS))
+    rows = pl.pallas_call(
+        advance_kernel,
+        out_shape=shape(K, COLS, COLS),
+        compiler_params=small(8),
+        cost_estimate=busy(3),
+        name="advance",
+    )(ext)
+    bred, scaled, sums = main_call(rows, strips, *got, *weights)
     sums = spread(spread(sums, FLAT), DEEP)
     analysis, perturb = pl.pallas_call(
         functools.partial(final_kernel, cells_all, obs_all),

time: 97.8 us -> 92 us (0.941)
  waiting for transfers between devices: 6.41 us -> 0.02 us
  local copies, waits for them, and re-layouts: 1.83 us -> 4.01 us
  Pallas kernels: 17.3 us -> 15.9 us
    ppermute x4, waiting for transfers between devices: 6.41 us -> 0.02 us  [the longest x2 0.01 us: swap(): other = lax.ppermute(packed[1], axes, second)]
    pallas_call x1 -> x3, Pallas kernels: 15.6 us -> 12.6 us  [the longest x1 8.08 us: main_call(): pl.pallas_call(main_kernel, out_shape=(shape(K * PLANES, ROWS, COLS), sha...]
    unnamed x10 -> x12, local copies, waits for them, and re-layouts: 1.8 us -> 3.98 us
    pallas_call x1, Pallas kernels: 0.31 us -> 1.99 us  [local(): pl.pallas_call(pack_cols_kernel, out_shape=(shape(FIELDS, 2 * ROWS, COLS)...]
  transfers between devices with their start and end apart: 4 -> 4, of which waited for: 2 -> 0; matrix products, arithmetic and copies ran while one was open for 0% -> 0% of each run, Pallas kernels for 0% -> 5%
where the time goes in v2:
time: 92 us; the launch traced here: 91.5 us
  blocking collectives  44.7 us (49%)
  starting transfers between devices  26 us (28%)
  Pallas kernels  15.9 us (17%)
  local copies, waits for them, and re-layouts  4.01 us (4%)
    all_to_all x2, blocking collectives, spread(): return lax.all_to_all(copies, axes, 0, 0, tiled=True).sum(axis=0)  44.7 us
    ppermute x2, starting transfers between devices, swap(): other = lax.ppermute(packed[1], axes, second)  17.1 us
    ppermute x2, starting transfers between devices, swap(): return (lax.ppermute(packed[0], axes, first), other)  8.88 us
    pallas_call x1, Pallas kernels, main_call(): pl.pallas_call(main_kernel, out_shape=(shape(K * PLANES, ROWS, COLS), sha...  8.08 us
    unnamed x12, local copies, waits for them, and re-layouts  3.98 us
    pallas_call x1, Pallas kernels, local(): pl.pallas_call(advance_kernel, out_shape=shape(K, COLS, COLS), compiler_p...  2.97 us
    pallas_call x1, Pallas kernels, local(): pl.pallas_call(pack_cols_kernel, out_shape=(shape(FIELDS, 2 * ROWS, COLS)...  1.99 us
  transfers between devices with their start and end apart: 4, of which 0 were waited for; matrix products, arithmetic and copies ran while one was open for 0% of the time, Pallas kernels for 5%

profile of v2, /device:TPU:1, one launch (start us, length us, event | category | flops | bytes accessed | tf_op | source)
XLA Modules:
  0.0 91.5 jit_solution(7347937543516567731)
XLA Ops:
  0.6 0.0 copy-start
  0.6 1.0 %copy-done = f32[8,3,4,8,128]{4,3,2,1,0:T(8,128)S(1)} copy-done((f32[8,3,4,8,128]{4,3,2,1,0:T(8,128)S(1)}, f32[8,3,4,8,128]{4,3,2,1,0:T(8,128)}, u32[]{:S(2)}) %copy-start) | copy-done | bytes 393240
  1.6 0.0 copy-start.2
  1.6 0.8 copy-done.2
  2.4 0.1 pack_rows.1
  2.5 4.0 %collective-permute-start = (f32[54,8,128]{2,1,0:T(8,128)S(1)}, f32[54,8,128]{2,1,0:T(8,128)S(1)}, u32[]{:S(2)}, u32[]{:S(2)}) collective-permute-start(f32[54,8,128]{2,1,0:T(8,128)S(1)} %get-tuple-element.16), channel_id=1, source_target_pairs={{0,16},{16,0},{32,48},{48,32},{64,80},{80,64},{96,112},{112,96},{1... | collective-permute-start | bytes 663560 | tf_op jit(solution)/shard_map/ppermute | solution.py:401
  6.5 14.5 %collective-permute-start.1 = (f32[54,8,128]{2,1,0:T(8,128)S(1)}, f32[54,8,128]{2,1,0:T(8,128)S(1)}, u32[]{:S(2)}, u32[]{:S(2)}) collective-permute-start(f32[54,8,128]{2,1,0:T(8,128)S(1)} %get-tuple-element.17), channel_id=1, source_target_pairs={{496,0},{0,496},{16,32},{32,16},{48,64},{64,48},{80,96},{96,80},{1... | collective-permute-start | bytes 663560 | tf_op jit(solution)/shard_map/ppermute | solution.py:400
  21.0 0.0 copy-start.3
  21.0 0.7 copy-done.3
  21.8 0.0 copy-start.4
  21.8 0.7 copy-done.4
  22.5 0.0 copy-start.5
  22.5 0.7 copy-done.5
  23.2 0.0 copy-start.1
  23.2 1.6 %weights.1 = (bf16[256,4096]{1,0:T(8,128)(2,1)S(1)}, f32[128,4096]{1,0:T(8,128)S(1)}, f32[2,4096]{1,0:T(2,128)S(1)}) custom-call(s32[1,4096]{1,0:T(1,128)S(1)} %bitcast.15, f32[2,4096]{1,0:T(2,128)S(1)} %copy-done.3, f32[1,4096]{1,0:T(1,128)S(1)} %bitcast.16), custom_call_target="tpu_custom_call" | custom-call | flops 3000000000 | tf_op jit(solution)/shard_map/weights/pallas_call | solution.py:447
  24.8 0.0 collective-permute-done.got_one
  24.8 0.0 collective-permute-done.1.got_two
  24.8 0.0 copy-done.1
  24.8 2.0 %pack_cols.1 = (f32[108,16,128]{2,1,0:T(8,128)S(1)}, f32[28,16,128]{2,1,0:T(8,128)S(1)}, f32[4,16,128]{2,1,0:T(8,128)S(1)}, f32[4,16,128]{2,1,0:T(8,128)S(1)}) custom-call(f32[96,8,128]{2,1,0:T(8,128)S(1)} %bitcast.10, f32[12,8,128]{2,1,0:T(8,128)S(1)} %bitcast.12, f32[54,8,128]{2,1,0:T(8,128)S(1)} %collective-permute-done.got_one, ...), custom_call_target="tpu_custom_call" | custom-call | tf_op jit(solution)/shard_map/pack_cols/pallas_call | solution.py:456
  26.8 4.9 %collective-permute-start.2 = (f32[4,16,128]{2,1,0:T(8,128)S(1)}, f32[4,16,128]{2,1,0:T(8,128)S(1)}, u32[]{:S(2)}, u32[]{:S(2)}) collective-permute-start(f32[4,16,128]{2,1,0:T(8,128)S(1)} %get-tuple-element.20), channel_id=1, source_target_pairs={{0,1},{1,0},{2,3},{3,2},{4,5},{5,4},{6,7},{7,6},{8,9},{9,8},{10,11... | collective-permute-start | bytes 98312 | tf_op jit(solution)/shard_map/ppermute | solution.py:401
  31.7 2.6 %collective-permute-start.3 = (f32[4,16,128]{2,1,0:T(8,128)S(1)}, f32[4,16,128]{2,1,0:T(8,128)S(1)}, u32[]{:S(2)}, u32[]{:S(2)}) collective-permute-start(f32[4,16,128]{2,1,0:T(8,128)S(1)} %get-tuple-element.21), channel_id=1, source_target_pairs={{15,0},{0,15},{1,2},{2,1},{3,4},{4,3},{5,6},{6,5},{7,8},{8,7},{9,1... | collective-permute-start | bytes 98312 | tf_op jit(solution)/shard_map/ppermute | solution.py:400
  34.3 3.0 %advance.1.rows_ref = f32[8,128,128]{2,1,0:T(8,128)S(1)} custom-call(f32[108,16,128]{2,1,0:T(8,128)S(1)} %get-tuple-element.18.ext_ref), custom_call_target="tpu_custom_call" | custom-call | flops 3000000000 | tf_op jit(solution)/shard_map/advance/pallas_call | solution.py:464
  37.3 0.0 collective-permute-done.2.got_one
  37.3 0.0 collective-permute-done.3.got_two
  37.3 8.1 %advance_sample.1 = (f32[96,8,128]{2,1,0:T(8,128)S(1)}, f32[8,4096]{1,0:T(8,128)S(1)}, f32[1,128]{1,0:T(1,128)S(1)}) custom-call(f32[8,128,128]{2,1,0:T(8,128)S(1)} %advance.1.rows_ref, f32[28,16,128]{2,1,0:T(8,128)S(1)} %get-tuple-element.19.strip_ref, f32[4,16,128]{2,1,0:T(8,128)S(1)} %collective-permute-done.2.got_one, ...), custom_call_target="tpu_custom_call" | custom-call | tf_op jit(solution)/shard_map/advance_sample/pallas_call | solution.py:415
  45.4 22.3 %all_to_all.10 = f32[32,1,128]{2,1,0:T(1,128)S(1)} all-to-all(f32[32,1,128]{2,1,0:T(1,128)S(1)} %broadcast_in_dim.7), channel_id=1, replica_groups=mesh['z_lo'=8,'y'=4,'z_hi'=2,'x'=4,'core'=2] {'y','x','core'}, dimensions={0} | all-to-all | bytes 32768 | tf_op jit(solution)/shard_map/all_to_all | solution.py:411
  67.8 22.4 %all_to_all.11 = f32[16,1,128]{2,1,0:T(1,128)S(1)} all-to-all(f32[16,1,128]{2,1,0:T(1,128)S(1)} %broadcast_in_dim.16), channel_id=1, replica_groups=mesh['z_lo'=8,'y'=4,'z_hi'=2,'x'=4,'core'=2] {'z_lo','z_hi'}, dimensions={0} | all-to-all | bytes 16384 | tf_op jit(solution)/shard_map/all_to_all | solution.py:411
  90.2 1.3 %combine.1 = (f32[96,8,128]{2,1,0:T(8,128)}, f32[8,4096]{1,0:T(8,128)}) custom-call(f32[1,128]{1,0:T(1,128)S(1)} %bitcast.13, f32[96,8,128]{2,1,0:T(8,128)S(1)} %get-tuple-element.26.bred_ref, f32[8,4096]{1,0:T(8,128)S(1)} %get-tuple-element.27.scaled_ref), custom_call_target="tpu_custom_call" | custom-call | tf_op jit(solution)/shard_map/combine/pallas_call | solution.py:473
  (4 shorter events, 0.1 us)
Async XLA Ops:
  0.6 1.0 %copy-start = (f32[8,3,4,8,128]{4,3,2,1,0:T(8,128)S(1)}, f32[8,3,4,8,128]{4,3,2,1,0:T(8,128)}, u32[]{:S(2)}) copy-start(f32[8,3,4,8,128]{4,3,2,1,0:T(8,128)} %param.5) | copy-start | bytes 1179652
  1.6 0.8 copy-start.2
  2.5 22.3 %collective-permute-start = (f32[54,8,128]{2,1,0:T(8,128)S(1)}, f32[54,8,128]{2,1,0:T(8,128)S(1)}, u32[]{:S(2)}, u32[]{:S(2)}) collective-permute-start(f32[54,8,128]{2,1,0:T(8,128)S(1)} %get-tuple-element.16), channel_id=1, source_target_pairs={{0,16},{16,0},{32,48},{48,32},{64,80},{80,64},{96,112},{112,96},{1... | collective-permute-start | bytes 663560 | tf_op jit(solution)/shard_map/ppermute | solution.py:401
  6.5 18.3 %collective-permute-start.1 = (f32[54,8,128]{2,1,0:T(8,128)S(1)}, f32[54,8,128]{2,1,0:T(8,128)S(1)}, u32[]{:S(2)}, u32[]{:S(2)}) collective-permute-start(f32[54,8,128]{2,1,0:T(8,128)S(1)} %get-tuple-element.17), channel_id=1, source_target_pairs={{496,0},{0,496},{16,32},{32,16},{48,64},{64,48},{80,96},{96,80},{1... | collective-permute-start | bytes 663560 | tf_op jit(solution)/shard_map/ppermute | solution.py:400
  21.0 0.8 copy-start.3
  21.8 0.7 copy-start.4
  22.5 0.7 copy-start.5
  23.2 1.6 %copy-start.1 = (f32[8,3,4,8,128]{4,3,2,1,0:T(8,128)S(1)}, f32[8,3,4,8,128]{4,3,2,1,0:T(8,128)}, u32[]{:S(2)}) copy-start(f32[8,3,4,8,128]{4,3,2,1,0:T(8,128)} %param.5) | copy-start | bytes 1179652
  26.8 10.5 %collective-permute-start.2 = (f32[4,16,128]{2,1,0:T(8,128)S(1)}, f32[4,16,128]{2,1,0:T(8,128)S(1)}, u32[]{:S(2)}, u32[]{:S(2)}) collective-permute-start(f32[4,16,128]{2,1,0:T(8,128)S(1)} %get-tuple-element.20), channel_id=1, source_target_pairs={{0,1},{1,0},{2,3},{3,2},{4,5},{5,4},{6,7},{7,6},{8,9},{9,8},{10,11... | collective-permute-start | bytes 98312 | tf_op jit(solution)/shard_map/ppermute | solution.py:401
  31.7 5.6 %collective-permute-start.3 = (f32[4,16,128]{2,1,0:T(8,128)S(1)}, f32[4,16,128]{2,1,0:T(8,128)S(1)}, u32[]{:S(2)}, u32[]{:S(2)}) collective-permute-start(f32[4,16,128]{2,1,0:T(8,128)S(1)} %get-tuple-element.21), channel_id=1, source_target_pairs={{15,0},{0,15},{1,2},{2,1},{3,4},{4,3},{5,6},{6,5},{7,8},{8,7},{9,1... | collective-permute-start | bytes 98312 | tf_op jit(solution)/shard_map/ppermute | solution.py:400

commit v3 on v2

--- a/solution.py
+++ b/solution.py
@@ -49,7 +49,7 @@
     return lax.axis_index("core") == 1
 
 
-def pack_rows_kernel(vec_ref, back_ref, one_ref, two_ref, all_ref):
+def pack_rows_kernel(vec_ref, back_ref, all_ref, one_ref, two_ref):
     odd = odd_row()
     all_ref[0 : K * PLANES] = vec_ref[...]
     all_ref[K * PLANES : FIELDS] = back_ref[...]
@@ -62,11 +62,10 @@
     two_ref[...] = jnp.where(odd, up, down)
 
 
-def pack_cols_kernel(vec_ref, back_ref, got_one, got_two, ext_ref, strip_ref, one_ref, two_ref):
+def pack_cols_kernel(own_ref, got_one, got_two, ext_ref, strip_ref, one_ref, two_ref):
     at_odd_row = odd_row()
     at_odd_col = odd_col()
-    ext_ref[0 : K * PLANES, 0:ROWS] = vec_ref[...]
-    ext_ref[K * PLANES : FIELDS, 0:ROWS] = back_ref[...]
+    ext_ref[:, 0:ROWS] = own_ref[...]
     top = iota((HALF, ROWS, COLS), 1) < 4
     low = jnp.where(at_odd_row, got_one[...], got_two[...])
     high = jnp.where(at_odd_row, got_two[...], got_one[...])
@@ -77,20 +76,23 @@
     for group in range(GROUPS):
         up = jnp.zeros((2 * ROWS, COLS), F32)
         down = jnp.zeros((2 * ROWS, COLS), F32)
-        for u in range(8):
-            t = group * 8 + u
-            if t >= STRIPS:
-                break
+        first, last = group * 8, min(group * 8 + 8, STRIPS)
+        planes = {f: ext_ref[f] for t in range(first, last) for f in strip_fields(t)}
+        strips = []
+        for t in range(first, last):
+            u = t - first
             strip = jnp.zeros((2 * ROWS, COLS), F32)
             for kk, field in enumerate(strip_fields(t)):
-                plane = ext_ref[field]
+                plane = planes[field]
                 left = (lane >= 32 * kk + 4) & (lane < 32 * kk + 16)
                 right = (lane >= 32 * kk + 16) & (lane < 32 * kk + 28)
                 strip = jnp.where(left, roll(plane, 32 * kk + 4, 1), strip)
                 strip = jnp.where(right, roll(plane, 32 * kk + 28, 1), strip)
-            strip_ref[t] = strip
+            strips.append(strip)
             down = jnp.where(eighth == u, roll(strip, 4 * u - 4, 1), down)
             up = jnp.where(eighth == u, roll(strip, 4 * u - 24, 1), up)
+        for t, strip in zip(range(first, last), strips):
+            strip_ref[t] = strip
         one_ref[group] = jnp.where(at_odd_col, down, up)
         two_ref[group] = jnp.where(at_odd_col, up, down)
 
@@ -136,7 +138,7 @@
     ref[k, OWN + PLANES + plane : OWN + PLANES + plane + 1] = field[ROWS : ROWS + 1]
 
 
-def advance_kernel(ext_ref, rows_ref):
+def advance_kernel(ext_ref, rows_ref, table_ref):
     rows_ref[:, OWN + 2 * PLANES :] = jnp.zeros((K, COLS - OWN - 2 * PLANES, COLS), F32)
     for level in range(L):
         base = K * PLANES + level
@@ -156,6 +158,17 @@
             return carry
 
         lax.fori_loop(0, K // BATCH, body, 0)
+    inner = iota((COLS, COLS), 1)
+    inner = (inner >= 3) & (inner < COLS - 3)
+    for k in range(K):
+        put_table(table_ref, k * COLS, jnp.where(inner, rows_ref[k], 0.0).T)
+
+
+def put_table(ref, at, value):
+    high = value.astype(jnp.bfloat16)
+    low = (value - high.astype(F32)).astype(jnp.bfloat16)
+    ref[at : at + value.shape[0], 0:COLS] = high
+    ref[at : at + value.shape[0], COLS : 2 * COLS] = low
 
 
 def weights_kernel(site_ref, off_ref, err_ref, pick_ref, weight_ref, ends_ref):
@@ -195,17 +208,18 @@
         weight_ref[:, at] = jnp.where(
             index == col, own_y, jnp.where(index == next_col, side_y, 0.0)
         )
-        ends_ref[0:1, at] = jnp.where(next_col == -1, side_y, 0.0)
-        ends_ref[1:2, at] = jnp.where(next_col == COLS, side_y, 0.0)
+        line = iota((ROWS, CHUNK), 0)
+        line = jnp.where(line < 4, line - 1, line + COLS - 7)
+        ends_ref[:, at] = jnp.where(line == col, own_y, jnp.where(line == next_col, side_y, 0.0))
         return carry
 
     lax.fori_loop(0, OBS // CHUNK, step, 0)
 
 
 def main_kernel(
-    rows_ref, strip_ref, got_one, got_two, pick_ref, weight_ref, ends_ref,
+    rows_ref, table_ref, strip_ref, got_one, got_two, pick_ref, weight_ref, ends_ref,
     bred_ref, scaled_ref, sums_ref,
-    whole_ref, side_ref, table_ref, pair_ref,
+    whole_ref, side_ref, edge_ref, pair_ref,
 ):
     at_odd_col = odd_col()
     lane = iota((2 * ROWS, COLS), 1)
@@ -220,6 +234,7 @@
             strip = jnp.where(eighth == 0, roll(left, -4 * u, 1), strip_ref[t])
             whole_ref[t] = jnp.where(eighth == 7, roll(right, 28 - 4 * u, 1), strip)
     side_ref[:, OWN + 2 * PLANES :] = jnp.zeros((2, COLS - OWN - 2 * PLANES, COLS), F32)
+    results = []
     for level in range(L):
         mixed_back = whole_ref[2 * PLANES + level]
         back = []
@@ -234,28 +249,27 @@
         start = [
             whole_ref[2 * (c * L + level) : 2 * (c * L + level) + 2] for c in range(3)
         ]
-        done = advance(start, back)
+        results.append(advance(start, back))
+    for level in range(L):
         for c in range(3):
             for half in range(2):
-                put_rows(side_ref, half, c * L + level, done[c][half])
-
-    def put(at, count, value):
-        high = value.astype(jnp.bfloat16)
-        low = (value - high.astype(F32)).astype(jnp.bfloat16)
-        table_ref[at : at + count, 0:COLS] = high
-        table_ref[at : at + count, COLS : 2 * COLS] = low
-
-    lane = iota((COLS, COLS), 1)
+                put_rows(side_ref, half, c * L + level, results[level][c][half])
+
+    across = [side_ref[half].T for half in range(2)]
+    lines = []
     for k in range(K):
-        side, kk = side_ref[k // 4], k % 4
-        fields = jnp.where(lane < 3, roll(side, -(32 * kk + 4), 1), rows_ref[k])
-        fields = jnp.where(lane >= COLS - 3, roll(side, 100 - 32 * kk, 1), fields)
-        bred_ref[k * PLANES : (k + 1) * PLANES] = fields[:OWN].reshape(PLANES, ROWS, COLS)
-        put(k * COLS, COLS, fields.T)
-    across = [side_ref[half].T for half in range(2)]
-    lines = [across[k // 4][32 * (k % 4) + 3 :][:1] for k in range(K)]
-    lines += [across[k // 4][32 * (k % 4) + 28 :][:1] for k in range(K)]
-    put(K * COLS, 2 * K, jnp.concatenate(lines, axis=0))
+        turned, at = across[k // 4], 32 * (k % 4)
+        lines += [turned[at + 3 : at + 7], turned[at + 25 : at + 29]]
+    put_table(edge_ref, 0, jnp.concatenate(lines, axis=0))
+    lane = iota((OWN, COLS), 1)
+    for pair in range(0, K, 2):
+        fields = []
+        for k in (pair, pair + 1):
+            side, kk = side_ref[k // 4, 0:OWN], k % 4
+            field = jnp.where(lane < 3, roll(side, -(32 * kk + 4), 1), rows_ref[k, 0:OWN])
+            fields.append(jnp.where(lane >= COLS - 3, roll(side, 100 - 32 * kk, 1), field))
+        for k, field in zip((pair, pair + 1), fields):
+            bred_ref[k * PLANES : (k + 1) * PLANES] = field.reshape(PLANES, ROWS, COLS)
 
     for i in range(K):
         mine = bred_ref[i * PLANES : (i + 1) * PLANES]
@@ -279,20 +293,19 @@
         low2 = jnp.concatenate([low, low], axis=0)
         weight = weight_ref[:, at]
 
-        def mixed(start, count):
-            part = table_ref[start : start + count]
+        def mixed(part):
             return jnp.dot(part, high2, preferred_element_type=F32) + jnp.dot(
                 part, low2, preferred_element_type=F32
             )
 
         out = jnp.zeros((K, CHUNK), F32)
         sub = iota((K, CHUNK), 0)
+        ends = mixed(edge_ref[...])
         for k in range(K):
-            line = jnp.sum(mixed(k * COLS, COLS) * weight, axis=0, keepdims=True)
-            out = jnp.where(sub == k, line, out)
-        ends_at = mixed(K * COLS, 2 * K)
-        out = out + ends_at[:K] * ends_ref[0:1, at]
-        out = out + ends_at[K:] * ends_ref[1:2, at]
+            part = mixed(table_ref[k * COLS : (k + 1) * COLS]) * weight
+            part = part.reshape(COLS // ROWS, ROWS, CHUNK).sum(axis=0)
+            part = part + ends[k * ROWS : (k + 1) * ROWS] * ends_ref[:, at]
+            out = jnp.where(sub == k, jnp.sum(part, axis=0, keepdims=True), out)
         scaled_ref[:, at] = out
         return carry
 
@@ -397,8 +410,9 @@
     count = lax.axis_size(axes)
     first = [(i, i ^ 1) for i in range(count)]
     second = [((i - 1) % count, ((i ^ 1) - 1) % count) for i in range(count)]
-    other = lax.ppermute(packed[1], axes, second)
-    return lax.ppermute(packed[0], axes, first), other
+    far = lax.ppermute(packed[1], axes, second)
+    near = lax.ppermute(packed[0], axes, first)
+    return near, far
 
 
 def small(mib):
@@ -418,7 +432,7 @@
         scratch_shapes=[
             pltpu.VMEM((STRIPS, 2 * ROWS, COLS), F32),
             pltpu.VMEM((2, COLS, COLS), F32),
-            pltpu.VMEM((K * COLS + 2 * K, 2 * COLS), jnp.bfloat16),
+            pltpu.VMEM((K * ROWS, 2 * COLS), jnp.bfloat16),
             pltpu.VMEM((COLS, COLS), F32),
         ],
         compiler_params=small(16),
@@ -436,10 +450,9 @@
     obs_all = float(OBS * devices_all)
     vec = vectors.reshape(K * PLANES, ROWS, COLS)
     back = background.reshape(PLANES, ROWS, COLS)
-    packed = pl.pallas_call(
+    own, *packed = pl.pallas_call(
         pack_rows_kernel,
-        out_shape=(shape(HALF, ROWS, COLS),) * 2,
-        scratch_shapes=[pltpu.VMEM((FIELDS, ROWS, COLS), F32)],
+        out_shape=(shape(FIELDS, ROWS, COLS),) + (shape(HALF, ROWS, COLS),) * 2,
         compiler_params=small(8),
         name="pack_rows",
     )(vec, back)
@@ -447,7 +460,7 @@
     weights = pl.pallas_call(
         weights_kernel,
         out_shape=(
-            jax.ShapeDtypeStruct((2 * COLS, OBS), jnp.bfloat16), shape(COLS, OBS), shape(2, OBS)
+            jax.ShapeDtypeStruct((2 * COLS, OBS), jnp.bfloat16), shape(COLS, OBS), shape(ROWS, OBS)
         ),
         compiler_params=small(8),
         cost_estimate=busy(3),
@@ -459,16 +472,18 @@
         + (shape(GROUPS, 2 * ROWS, COLS),) * 2,
         compiler_params=small(8),
         name="pack_cols",
-    )(vec, back, *got)
+    )(own, *got)
     got = swap(packed, GY)
-    rows = pl.pallas_call(
+    mine = pl.pallas_call(
         advance_kernel,
-        out_shape=shape(K, COLS, COLS),
+        out_shape=(
+            shape(K, COLS, COLS), jax.ShapeDtypeStruct((K * COLS, 2 * COLS), jnp.bfloat16)
+        ),
         compiler_params=small(8),
         cost_estimate=busy(3),
         name="advance",
     )(ext)
-    bred, scaled, sums = main_call(rows, strips, *got, *weights)
+    bred, scaled, sums = main_call(*mine, strips, *got, *weights)
     sums = spread(spread(sums, FLAT), DEEP)
     analysis, perturb = pl.pallas_call(
         functools.partial(final_kernel, cells_all, obs_all),

time: 92 us -> 92.2 us (level)
    unnamed x12 -> x10, local copies, waits for them, and re-layouts: 3.98 us -> 3.97 us
  transfers between devices with their start and end apart: 4 -> 4, of which waited for: 0 -> 1; matrix products, arithmetic and copies ran while one was open for 0% -> 0% of each run, Pallas kernels for 5% -> 5%
where the time goes in v3:
time: 92.2 us; the launch traced here: 91.7 us
  blocking collectives  44.5 us (48%)
  starting transfers between devices  26 us (28%)
  Pallas kernels  16.3 us (18%)
  local copies, waits for them, and re-layouts  4.01 us (4%)
    all_to_all x2, blocking collectives, spread(): return lax.all_to_all(copies, axes, 0, 0, tiled=True).sum(axis=0)  44.5 us
    ppermute x2, starting transfers between devices, swap(): far = lax.ppermute(packed[1], axes, second)  17.1 us
    ppermute x2, starting transfers between devices, swap(): near = lax.ppermute(packed[0], axes, first)  8.89 us
    pallas_call x1, Pallas kernels, main_call(): pl.pallas_call(main_kernel, out_shape=(shape(K * PLANES, ROWS, COLS), sha...  8.28 us
    unnamed x10, local copies, waits for them, and re-layouts  3.97 us
    pallas_call x1, Pallas kernels, local(): pl.pallas_call(advance_kernel, out_shape=(shape(K, COLS, COLS), jax.Shape...  3.18 us
    pallas_call x1, Pallas kernels, local(): pl.pallas_call(pack_cols_kernel, out_shape=(shape(FIELDS, 2 * ROWS, COLS)...  1.98 us
  transfers between devices with their start and end apart: 4, of which 1 were waited for; matrix products, arithmetic and copies ran while one was open for 0% of the time, Pallas kernels for 5%

profile of v3, /device:TPU:1, one launch (start us, length us, event | category | flops | bytes accessed | tf_op | source)
XLA Modules:
  0.0 91.7 jit_solution(2392421471645222938)
XLA Ops:
  0.6 0.0 copy-start
  0.6 1.0 %copy-done = f32[8,3,4,8,128]{4,3,2,1,0:T(8,128)S(1)} copy-done((f32[8,3,4,8,128]{4,3,2,1,0:T(8,128)S(1)}, f32[8,3,4,8,128]{4,3,2,1,0:T(8,128)}, u32[]{:S(2)}) %copy-start) | copy-done | bytes 393240
  1.6 0.0 copy-start.1
  1.6 0.8 copy-done.1
  2.4 0.1 pack_rows.1
  2.5 4.0 %collective-permute-start = (f32[54,8,128]{2,1,0:T(8,128)S(1)}, f32[54,8,128]{2,1,0:T(8,128)S(1)}, u32[]{:S(2)}, u32[]{:S(2)}) collective-permute-start(f32[54,8,128]{2,1,0:T(8,128)S(1)} %get-tuple-element.20), channel_id=1, source_target_pairs={{0,16},{16,0},{32,48},{48,32},{64,80},{80,64},{96,112},{112,96},{1... | collective-permute-start | bytes 663560 | tf_op jit(solution)/shard_map/ppermute | solution.py:414
  6.6 14.5 %collective-permute-start.1 = (f32[54,8,128]{2,1,0:T(8,128)S(1)}, f32[54,8,128]{2,1,0:T(8,128)S(1)}, u32[]{:S(2)}, u32[]{:S(2)}) collective-permute-start(f32[54,8,128]{2,1,0:T(8,128)S(1)} %get-tuple-element.21), channel_id=1, source_target_pairs={{496,0},{0,496},{16,32},{32,16},{48,64},{64,48},{80,96},{96,80},{1... | collective-permute-start | bytes 663560 | tf_op jit(solution)/shard_map/ppermute | solution.py:413
  21.1 0.0 copy-start.2
  21.1 0.7 copy-done.2
  21.8 0.0 copy-start.3
  21.8 0.7 copy-done.3
  22.6 0.0 copy-start.4
  22.6 0.7 copy-done.4
  23.3 1.5 %weights.1 = (bf16[256,4096]{1,0:T(8,128)(2,1)S(1)}, f32[128,4096]{1,0:T(8,128)S(1)}, f32[8,4096]{1,0:T(8,128)S(1)}) custom-call(s32[1,4096]{1,0:T(1,128)S(1)} %bitcast.13, f32[2,4096]{1,0:T(2,128)S(1)} %copy-done.2, f32[1,4096]{1,0:T(1,128)S(1)} %bitcast.14), custom_call_target="tpu_custom_call" | custom-call | flops 3000000000 | tf_op jit(solution)/shard_map/weights/pallas_call | solution.py:460
  24.8 0.0 collective-permute-done.got_one
  24.8 0.1 collective-permute-done.1.got_two
  24.9 2.0 %pack_cols.1 = (f32[108,16,128]{2,1,0:T(8,128)S(1)}, f32[28,16,128]{2,1,0:T(8,128)S(1)}, f32[4,16,128]{2,1,0:T(8,128)S(1)}, f32[4,16,128]{2,1,0:T(8,128)S(1)}) custom-call(f32[108,8,128]{2,1,0:T(8,128)S(1)} %get-tuple-element.19.own_ref, f32[54,8,128]{2,1,0:T(8,128)S(1)} %collective-permute-done.got_one, f32[54,8,128]{2,1,0:T(8,128)S(1)} %collective-permute-done.1.got_two), custom_call_target="tpu_custom_call" | custom-call | tf_op jit(solution)/shard_map/pack_cols/pallas_call | solution.py:469
  26.9 4.9 %collective-permute-start.2 = (f32[4,16,128]{2,1,0:T(8,128)S(1)}, f32[4,16,128]{2,1,0:T(8,128)S(1)}, u32[]{:S(2)}, u32[]{:S(2)}) collective-permute-start(f32[4,16,128]{2,1,0:T(8,128)S(1)} %get-tuple-element.26), channel_id=1, source_target_pairs={{0,1},{1,0},{2,3},{3,2},{4,5},{5,4},{6,7},{7,6},{8,9},{9,8},{10,11... | collective-permute-start | bytes 98312 | tf_op jit(solution)/shard_map/ppermute | solution.py:414
  31.8 2.6 %collective-permute-start.3 = (f32[4,16,128]{2,1,0:T(8,128)S(1)}, f32[4,16,128]{2,1,0:T(8,128)S(1)}, u32[]{:S(2)}, u32[]{:S(2)}) collective-permute-start(f32[4,16,128]{2,1,0:T(8,128)S(1)} %get-tuple-element.27), channel_id=1, source_target_pairs={{15,0},{0,15},{1,2},{2,1},{3,4},{4,3},{5,6},{6,5},{7,8},{8,7},{9,1... | collective-permute-start | bytes 98312 | tf_op jit(solution)/shard_map/ppermute | solution.py:413
  34.4 3.2 %advance.1 = (f32[8,128,128]{2,1,0:T(8,128)S(1)}, bf16[1024,256]{1,0:T(8,128)(2,1)S(1)}) custom-call(f32[108,16,128]{2,1,0:T(8,128)S(1)} %get-tuple-element.22.ext_ref), custom_call_target="tpu_custom_call" | custom-call | flops 3000000000 | tf_op jit(solution)/shard_map/advance/pallas_call | solution.py:477
  37.6 0.0 collective-permute-done.2.got_one
  37.6 0.0 collective-permute-done.3.got_two
  37.6 8.3 %advance_sample.1 = (f32[96,8,128]{2,1,0:T(8,128)S(1)}, f32[8,4096]{1,0:T(8,128)S(1)}, f32[1,128]{1,0:T(1,128)S(1)}) custom-call(f32[8,128,128]{2,1,0:T(8,128)S(1)} %get-tuple-element.23.rows_ref, bf16[1024,256]{1,0:T(8,128)(2,1)S(1)} %get-tuple-element.24.table_ref, f32[28,16,128]{2,1,0:T(8,128)S(1)} %get-tuple-element.25.strip_ref, ...), custom_call_target="tpu_custom_call" | custom-call | tf_op jit(solution)/shard_map/advance_sample/pallas_call | solution.py:429
  45.9 22.3 %all_to_all.10 = f32[32,1,128]{2,1,0:T(1,128)S(1)} all-to-all(f32[32,1,128]{2,1,0:T(1,128)S(1)} %broadcast_in_dim.7), channel_id=1, replica_groups=mesh['z_lo'=8,'y'=4,'z_hi'=2,'x'=4,'core'=2] {'y','x','core'}, dimensions={0} | all-to-all | bytes 32768 | tf_op jit(solution)/shard_map/all_to_all | solution.py:425
  68.2 22.2 %all_to_all.11 = f32[16,1,128]{2,1,0:T(1,128)S(1)} all-to-all(f32[16,1,128]{2,1,0:T(1,128)S(1)} %broadcast_in_dim.16), channel_id=1, replica_groups=mesh['z_lo'=8,'y'=4,'z_hi'=2,'x'=4,'core'=2] {'z_lo','z_hi'}, dimensions={0} | all-to-all | bytes 16384 | tf_op jit(solution)/shard_map/all_to_all | solution.py:425
  90.4 1.3 %combine.1 = (f32[96,8,128]{2,1,0:T(8,128)}, f32[8,4096]{1,0:T(8,128)}) custom-call(f32[1,128]{1,0:T(1,128)S(1)} %bitcast.11, f32[96,8,128]{2,1,0:T(8,128)S(1)} %get-tuple-element.32.bred_ref, f32[8,4096]{1,0:T(8,128)S(1)} %get-tuple-element.33.scaled_ref), custom_call_target="tpu_custom_call" | custom-call | tf_op jit(solution)/shard_map/combine/pallas_call | solution.py:488
  (4 shorter events, 0.1 us)
Async XLA Ops:
  0.6 1.0 %copy-start = (f32[8,3,4,8,128]{4,3,2,1,0:T(8,128)S(1)}, f32[8,3,4,8,128]{4,3,2,1,0:T(8,128)}, u32[]{:S(2)}) copy-start(f32[8,3,4,8,128]{4,3,2,1,0:T(8,128)} %param.5) | copy-start | bytes 1179652
  1.6 0.8 copy-start.1
  2.5 22.2 %collective-permute-start = (f32[54,8,128]{2,1,0:T(8,128)S(1)}, f32[54,8,128]{2,1,0:T(8,128)S(1)}, u32[]{:S(2)}, u32[]{:S(2)}) collective-permute-start(f32[54,8,128]{2,1,0:T(8,128)S(1)} %get-tuple-element.20), channel_id=1, source_target_pairs={{0,16},{16,0},{32,48},{48,32},{64,80},{80,64},{96,112},{112,96},{1... | collective-permute-start | bytes 663560 | tf_op jit(solution)/shard_map/ppermute | solution.py:414
  6.6 18.3 %collective-permute-start.1 = (f32[54,8,128]{2,1,0:T(8,128)S(1)}, f32[54,8,128]{2,1,0:T(8,128)S(1)}, u32[]{:S(2)}, u32[]{:S(2)}) collective-permute-start(f32[54,8,128]{2,1,0:T(8,128)S(1)} %get-tuple-element.21), channel_id=1, source_target_pairs={{496,0},{0,496},{16,32},{32,16},{48,64},{64,48},{80,96},{96,80},{1... | collective-permute-start | bytes 663560 | tf_op jit(solution)/shard_map/ppermute | solution.py:413
  21.1 0.8 copy-start.2
  21.8 0.7 copy-start.3
  22.6 0.7 copy-start.4
  26.9 10.7 %collective-permute-start.2 = (f32[4,16,128]{2,1,0:T(8,128)S(1)}, f32[4,16,128]{2,1,0:T(8,128)S(1)}, u32[]{:S(2)}, u32[]{:S(2)}) collective-permute-start(f32[4,16,128]{2,1,0:T(8,128)S(1)} %get-tuple-element.26), channel_id=1, source_target_pairs={{0,1},{1,0},{2,3},{3,2},{4,5},{5,4},{6,7},{7,6},{8,9},{9,8},{10,11... | collective-permute-start | bytes 98312 | tf_op jit(solution)/shard_map/ppermute | solution.py:414
  31.8 5.8 %collective-permute-start.3 = (f32[4,16,128]{2,1,0:T(8,128)S(1)}, f32[4,16,128]{2,1,0:T(8,128)S(1)}, u32[]{:S(2)}, u32[]{:S(2)}) collective-permute-start(f32[4,16,128]{2,1,0:T(8,128)S(1)} %get-tuple-element.27), channel_id=1, source_target_pairs={{15,0},{0,15},{1,2},{2,1},{3,4},{4,3},{5,6},{6,5},{7,8},{8,7},{9,1... | collective-permute-start | bytes 98312 | tf_op jit(solution)/shard_map/ppermute | solution.py:413

commit v4 on v3

--- a/solution.py
+++ b/solution.py
@@ -62,7 +62,7 @@
     two_ref[...] = jnp.where(odd, up, down)
 
 
-def pack_cols_kernel(own_ref, got_one, got_two, ext_ref, strip_ref, one_ref, two_ref):
+def pack_cols_kernel(own_ref, got_one, got_two, ext_ref, one_ref, two_ref):
     at_odd_row = odd_row()
     at_odd_col = odd_col()
     ext_ref[:, 0:ROWS] = own_ref[...]
@@ -72,27 +72,14 @@
     ext_ref[0:HALF, ROWS : 2 * ROWS] = jnp.where(top, high, low)
     ext_ref[HALF:FIELDS, ROWS : 2 * ROWS] = roll(jnp.where(top, low, high), 4, 1)
     lane = iota((2 * ROWS, COLS), 1)
-    eighth = lax.rem(lane, 32) // 4
     for group in range(GROUPS):
         up = jnp.zeros((2 * ROWS, COLS), F32)
         down = jnp.zeros((2 * ROWS, COLS), F32)
-        first, last = group * 8, min(group * 8 + 8, STRIPS)
-        planes = {f: ext_ref[f] for t in range(first, last) for f in strip_fields(t)}
-        strips = []
-        for t in range(first, last):
-            u = t - first
-            strip = jnp.zeros((2 * ROWS, COLS), F32)
-            for kk, field in enumerate(strip_fields(t)):
-                plane = planes[field]
-                left = (lane >= 32 * kk + 4) & (lane < 32 * kk + 16)
-                right = (lane >= 32 * kk + 16) & (lane < 32 * kk + 28)
-                strip = jnp.where(left, roll(plane, 32 * kk + 4, 1), strip)
-                strip = jnp.where(right, roll(plane, 32 * kk + 28, 1), strip)
-            strips.append(strip)
-            down = jnp.where(eighth == u, roll(strip, 4 * u - 4, 1), down)
-            up = jnp.where(eighth == u, roll(strip, 4 * u - 24, 1), up)
-        for t, strip in zip(range(first, last), strips):
-            strip_ref[t] = strip
+        for u in range(min(8, STRIPS - group * 8)):
+            for kk, field in enumerate(strip_fields(group * 8 + u)):
+                moved = roll(ext_ref[field], 32 * kk + 4 * u, 1)
+                down = jnp.where(lane // 4 == 8 * kk + u, moved, down)
+                up = jnp.where(lane // 4 == (8 * kk + u + 31) % 32, moved, up)
         one_ref[group] = jnp.where(at_odd_col, down, up)
         two_ref[group] = jnp.where(at_odd_col, up, down)
 
@@ -138,7 +125,15 @@
     ref[k, OWN + PLANES + plane : OWN + PLANES + plane + 1] = field[ROWS : ROWS + 1]
 
 
-def advance_kernel(ext_ref, rows_ref, table_ref):
+def inner_kernel(ext_ref, pick_ref, weight_ref, rows_ref, strip_ref, part_ref, table_ref):
+    lane = iota((2 * ROWS, COLS), 1)
+    for t in range(STRIPS):
+        strip = jnp.zeros((2 * ROWS, COLS), F32)
+        for kk, field in enumerate(strip_fields(t)):
+            plane = ext_ref[field]
+            strip = jnp.where(lane >= 32 * kk + 4, roll(plane, 32 * kk + 4, 1), strip)
+            strip = jnp.where(lane >= 32 * kk + 16, roll(plane, 32 * kk + 28, 1), strip)
+        strip_ref[t] = strip
     rows_ref[:, OWN + 2 * PLANES :] = jnp.zeros((K, COLS - OWN - 2 * PLANES, COLS), F32)
     for level in range(L):
         base = K * PLANES + level
@@ -162,6 +157,31 @@
     inner = (inner >= 3) & (inner < COLS - 3)
     for k in range(K):
         put_table(table_ref, k * COLS, jnp.where(inner, rows_ref[k], 0.0).T)
+
+    def sample(step, carry):
+        at, high2, low2 = picked(pick_ref, step)
+        weight = weight_ref[:, at]
+        out = jnp.zeros((K, CHUNK), F32)
+        sub = iota((K, CHUNK), 0)
+        for k in range(K):
+            part = mixed(table_ref[k * COLS : (k + 1) * COLS], high2, low2) * weight
+            out = jnp.where(sub == k, jnp.sum(part, axis=0, keepdims=True), out)
+        part_ref[:, at] = out
+        return carry
+
+    lax.fori_loop(0, OBS // CHUNK, sample, 0, unroll=True)
+
+
+def picked(pick_ref, step):
+    at = pl.ds(pl.multiple_of(step * CHUNK, CHUNK), CHUNK)
+    high, low = pick_ref[0:COLS, at], pick_ref[COLS : 2 * COLS, at]
+    return at, jnp.concatenate([high, high], axis=0), jnp.concatenate([low, low], axis=0)
+
+
+def mixed(part, high2, low2):
+    return jnp.dot(part, high2, preferred_element_type=F32) + jnp.dot(
+        part, low2, preferred_element_type=F32
+    )
 
 
 def put_table(ref, at, value):
@@ -217,13 +237,13 @@
 
 
 def main_kernel(
-    rows_ref, table_ref, strip_ref, got_one, got_two, pick_ref, weight_ref, ends_ref,
+    rows_ref, strip_ref, part_ref, got_one, got_two, pick_ref, ends_ref,
     bred_ref, scaled_ref, sums_ref,
     whole_ref, side_ref, edge_ref, pair_ref,
 ):
     at_odd_col = odd_col()
     lane = iota((2 * ROWS, COLS), 1)
-    eighth = lax.rem(lane, 32) // 4
+    eighth = (lane & 31) // 4
     for group in range(GROUPS):
         left = jnp.where(at_odd_col, got_one[group], got_two[group])
         right = jnp.where(at_odd_col, got_two[group], got_one[group])
@@ -231,7 +251,7 @@
             t = group * 8 + u
             if t >= STRIPS:
                 break
-            strip = jnp.where(eighth == 0, roll(left, -4 * u, 1), strip_ref[t])
+            strip = jnp.where(eighth == 0, roll(left, 4 - 4 * u, 1), strip_ref[t])
             whole_ref[t] = jnp.where(eighth == 7, roll(right, 28 - 4 * u, 1), strip)
     side_ref[:, OWN + 2 * PLANES :] = jnp.zeros((2, COLS - OWN - 2 * PLANES, COLS), F32)
     results = []
@@ -287,29 +307,17 @@
     )[0:1]
 
     def sample(step, carry):
-        at = pl.ds(pl.multiple_of(step * CHUNK, CHUNK), CHUNK)
-        high, low = pick_ref[0:COLS, at], pick_ref[COLS : 2 * COLS, at]
-        high2 = jnp.concatenate([high, high], axis=0)
-        low2 = jnp.concatenate([low, low], axis=0)
-        weight = weight_ref[:, at]
-
-        def mixed(part):
-            return jnp.dot(part, high2, preferred_element_type=F32) + jnp.dot(
-                part, low2, preferred_element_type=F32
-            )
-
-        out = jnp.zeros((K, CHUNK), F32)
+        at, high2, low2 = picked(pick_ref, step)
+        ends = mixed(edge_ref[...], high2, low2)
+        out = part_ref[:, at]
         sub = iota((K, CHUNK), 0)
-        ends = mixed(edge_ref[...])
         for k in range(K):
-            part = mixed(table_ref[k * COLS : (k + 1) * COLS]) * weight
-            part = part.reshape(COLS // ROWS, ROWS, CHUNK).sum(axis=0)
-            part = part + ends[k * ROWS : (k + 1) * ROWS] * ends_ref[:, at]
-            out = jnp.where(sub == k, jnp.sum(part, axis=0, keepdims=True), out)
+            part = ends[k * ROWS : (k + 1) * ROWS] * ends_ref[:, at]
+            out = jnp.where(sub == k, out + jnp.sum(part, axis=0, keepdims=True), out)
         scaled_ref[:, at] = out
         return carry
 
-    lax.fori_loop(0, OBS // CHUNK, sample, 0)
+    lax.fori_loop(0, OBS // CHUNK, sample, 0, unroll=True)
 
     scaled = scaled_ref[...]
     normal = lax.dot_general(
@@ -436,7 +444,7 @@
             pltpu.VMEM((COLS, COLS), F32),
         ],
         compiler_params=small(16),
-        name="advance_sample",
+        name="edges",
     )(*operands)
 
 
@@ -466,24 +474,23 @@
         cost_estimate=busy(3),
         name="weights",
     )(obs_site.reshape(1, OBS), obs_offset, obs_error.reshape(1, OBS))
-    ext, strips, *packed = pl.pallas_call(
+    ext, *packed = pl.pallas_call(
         pack_cols_kernel,
-        out_shape=(shape(FIELDS, 2 * ROWS, COLS), shape(STRIPS, 2 * ROWS, COLS))
-        + (shape(GROUPS, 2 * ROWS, COLS),) * 2,
+        out_shape=(shape(FIELDS, 2 * ROWS, COLS),) + (shape(GROUPS, 2 * ROWS, COLS),) * 2,
         compiler_params=small(8),
         name="pack_cols",
     )(own, *got)
     got = swap(packed, GY)
+    pick, weight, ends = weights
     mine = pl.pallas_call(
-        advance_kernel,
-        out_shape=(
-            shape(K, COLS, COLS), jax.ShapeDtypeStruct((K * COLS, 2 * COLS), jnp.bfloat16)
-        ),
-        compiler_params=small(8),
-        cost_estimate=busy(3),
-        name="advance",
-    )(ext)
-    bred, scaled, sums = main_call(*mine, strips, *got, *weights)
+        inner_kernel,
+        out_shape=(shape(K, COLS, COLS), shape(STRIPS, 2 * ROWS, COLS), shape(K, OBS)),
+        scratch_shapes=[pltpu.VMEM((K * COLS, 2 * COLS), jnp.bfloat16)],
+        compiler_params=small(16),
+        cost_estimate=busy(8),
+        name="inner",
+    )(ext, pick, weight)
+    bred, scaled, sums = main_call(*mine, *got, pick, ends)
     sums = spread(spread(sums, FLAT), DEEP)
     analysis, perturb = pl.pallas_call(
         functools.partial(final_kernel, cells_all, obs_all),

time: 92.2 us -> 84.6 us (0.918)
  blocking collectives: 44.5 us -> 39.6 us
  Pallas kernels: 16.3 us -> 13.6 us
    pallas_call x1, Pallas kernels: 8.28 us -> 2.27 us  [main_call(): pl.pallas_call(main_kernel, out_shape=(shape(K * PLANES, ROWS, COLS), sha...]
    all_to_all x2, blocking collectives: 44.5 us -> 39.6 us  [spread(): return lax.all_to_all(copies, axes, 0, 0, tiled=True).sum(axis=0)]
    pallas_call x1, Pallas kernels: 3.18 us -> 8.09 us  [local(): pl.pallas_call(inner_kernel, out_shape=(shape(K, COLS, COLS), shape(STRIP...]
    pallas_call x1, Pallas kernels: 1.98 us -> 0.32 us  [local(): pl.pallas_call(pack_cols_kernel, out_shape=(shape(FIELDS, 2 * ROWS, COLS)...]
  transfers between devices with their start and end apart: 4 -> 4, of which waited for: 1 -> 1; matrix products, arithmetic and copies ran while one was open for 0% -> 0% of each run, Pallas kernels for 5% -> 11%
where the time goes in v4:
time: 84.6 us; the launch traced here: 84 us
  blocking collectives  39.6 us (47%)
  starting transfers between devices  26 us (31%)
  Pallas kernels  13.6 us (16%)
  local copies, waits for them, and re-layouts  4.01 us (5%)
    all_to_all x2, blocking collectives, spread(): return lax.all_to_all(copies, axes, 0, 0, tiled=True).sum(axis=0)  39.6 us
    ppermute x2, starting transfers between devices, swap(): far = lax.ppermute(packed[1], axes, second)  17.1 us
    ppermute x2, starting transfers between devices, swap(): near = lax.ppermute(packed[0], axes, first)  8.89 us
    pallas_call x1, Pallas kernels, local(): pl.pallas_call(inner_kernel, out_shape=(shape(K, COLS, COLS), shape(STRIP...  8.09 us
    unnamed x10, local copies, waits for them, and re-layouts  3.97 us
    pallas_call x1, Pallas kernels, main_call(): pl.pallas_call(main_kernel, out_shape=(shape(K * PLANES, ROWS, COLS), sha...  2.27 us
  transfers between devices with their start and end apart: 4, of which 1 were waited for; matrix products, arithmetic and copies ran while one was open for 0% of the time, Pallas kernels for 11%

profile of v4, /device:TPU:1, one launch (start us, length us, event | category | flops | bytes accessed | tf_op | source)
XLA Modules:
  0.0 84.0 jit_solution(3254108807072768992)
XLA Ops:
  0.6 0.0 copy-start
  0.6 1.0 %copy-done = f32[8,3,4,8,128]{4,3,2,1,0:T(8,128)S(1)} copy-done((f32[8,3,4,8,128]{4,3,2,1,0:T(8,128)S(1)}, f32[8,3,4,8,128]{4,3,2,1,0:T(8,128)}, u32[]{:S(2)}) %copy-start) | copy-done | bytes 393240
  1.6 0.0 copy-start.1
  1.6 0.8 copy-done.1
  2.4 0.1 pack_rows.1
  2.5 4.0 %collective-permute-start = (f32[54,8,128]{2,1,0:T(8,128)S(1)}, f32[54,8,128]{2,1,0:T(8,128)S(1)}, u32[]{:S(2)}, u32[]{:S(2)}) collective-permute-start(f32[54,8,128]{2,1,0:T(8,128)S(1)} %get-tuple-element.20), channel_id=1, source_target_pairs={{0,16},{16,0},{32,48},{48,32},{64,80},{80,64},{96,112},{112,96},{1... | collective-permute-start | bytes 663560 | tf_op jit(solution)/shard_map/ppermute | solution.py:422
  6.6 14.5 %collective-permute-start.1 = (f32[54,8,128]{2,1,0:T(8,128)S(1)}, f32[54,8,128]{2,1,0:T(8,128)S(1)}, u32[]{:S(2)}, u32[]{:S(2)}) collective-permute-start(f32[54,8,128]{2,1,0:T(8,128)S(1)} %get-tuple-element.21), channel_id=1, source_target_pairs={{496,0},{0,496},{16,32},{32,16},{48,64},{64,48},{80,96},{96,80},{1... | collective-permute-start | bytes 663560 | tf_op jit(solution)/shard_map/ppermute | solution.py:421
  21.1 0.0 copy-start.2
  21.1 0.7 copy-done.2
  21.8 0.0 copy-start.3
  21.8 0.7 copy-done.3
  22.6 0.0 copy-start.4
  22.6 0.7 copy-done.4
  23.3 1.5 %weights.1 = (bf16[256,4096]{1,0:T(8,128)(2,1)S(1)}, f32[128,4096]{1,0:T(8,128)S(1)}, f32[8,4096]{1,0:T(8,128)S(1)}) custom-call(s32[1,4096]{1,0:T(1,128)S(1)} %bitcast.13, f32[2,4096]{1,0:T(2,128)S(1)} %copy-done.2, f32[1,4096]{1,0:T(1,128)S(1)} %bitcast.14), custom_call_target="tpu_custom_call" | custom-call | flops 3000000000 | tf_op jit(solution)/shard_map/weights/pallas_call | solution.py:468
  24.8 0.0 collective-permute-done.got_one
  24.8 0.1 collective-permute-done.1.got_two
  24.9 0.3 pack_cols.1
  25.2 4.9 %collective-permute-start.2 = (f32[4,16,128]{2,1,0:T(8,128)S(1)}, f32[4,16,128]{2,1,0:T(8,128)S(1)}, u32[]{:S(2)}, u32[]{:S(2)}) collective-permute-start(f32[4,16,128]{2,1,0:T(8,128)S(1)} %get-tuple-element.28), channel_id=1, source_target_pairs={{0,1},{1,0},{2,3},{3,2},{4,5},{5,4},{6,7},{7,6},{8,9},{9,8},{10,11... | collective-permute-start | bytes 98312 | tf_op jit(solution)/shard_map/ppermute | solution.py:422
  30.1 2.6 %collective-permute-start.3 = (f32[4,16,128]{2,1,0:T(8,128)S(1)}, f32[4,16,128]{2,1,0:T(8,128)S(1)}, u32[]{:S(2)}, u32[]{:S(2)}) collective-permute-start(f32[4,16,128]{2,1,0:T(8,128)S(1)} %get-tuple-element.29), channel_id=1, source_target_pairs={{15,0},{0,15},{1,2},{2,1},{3,4},{4,3},{5,6},{6,5},{7,8},{8,7},{9,1... | collective-permute-start | bytes 98312 | tf_op jit(solution)/shard_map/ppermute | solution.py:421
  32.7 8.1 %inner.1 = (f32[8,128,128]{2,1,0:T(8,128)S(1)}, f32[28,16,128]{2,1,0:T(8,128)S(1)}, f32[8,4096]{1,0:T(8,128)S(1)}) custom-call(f32[108,16,128]{2,1,0:T(8,128)S(1)} %get-tuple-element.22.ext_ref, bf16[256,4096]{1,0:T(8,128)(2,1)S(1)} %get-tuple-element.23.pick_ref, f32[128,4096]{1,0:T(8,128)S(1)} %get-tuple-element.24.weight_ref), custom_call_target="tpu_custom_call" | custom-call | flops 8000000000 | tf_op jit(solution)/shard_map/inner/pallas_call | solution.py:485
  40.8 0.0 collective-permute-done.2.got_one
  40.8 0.0 collective-permute-done.3.got_two
  40.8 2.3 %edges.1 = (f32[96,8,128]{2,1,0:T(8,128)S(1)}, f32[8,4096]{1,0:T(8,128)S(1)}, f32[1,128]{1,0:T(1,128)S(1)}) custom-call(f32[8,128,128]{2,1,0:T(8,128)S(1)} %get-tuple-element.25.rows_ref, f32[28,16,128]{2,1,0:T(8,128)S(1)} %get-tuple-element.26.strip_ref, f32[8,4096]{1,0:T(8,128)S(1)} %get-tuple-element.27.part_ref, ...), custom_call_target="tpu_custom_call" | custom-call | tf_op jit(solution)/shard_map/edges/pallas_call | solution.py:437
  43.1 22.3 %all_to_all.10 = f32[32,1,128]{2,1,0:T(1,128)S(1)} all-to-all(f32[32,1,128]{2,1,0:T(1,128)S(1)} %broadcast_in_dim.7), channel_id=1, replica_groups=mesh['z_lo'=8,'y'=4,'z_hi'=2,'x'=4,'core'=2] {'y','x','core'}, dimensions={0} | all-to-all | bytes 32768 | tf_op jit(solution)/shard_map/all_to_all | solution.py:433
  65.5 17.3 %all_to_all.11 = f32[16,1,128]{2,1,0:T(1,128)S(1)} all-to-all(f32[16,1,128]{2,1,0:T(1,128)S(1)} %broadcast_in_dim.16), channel_id=1, replica_groups=mesh['z_lo'=8,'y'=4,'z_hi'=2,'x'=4,'core'=2] {'z_lo','z_hi'}, dimensions={0} | all-to-all | bytes 16384 | tf_op jit(solution)/shard_map/all_to_all | solution.py:433
  82.7 1.3 %combine.1 = (f32[96,8,128]{2,1,0:T(8,128)}, f32[8,4096]{1,0:T(8,128)}) custom-call(f32[1,128]{1,0:T(1,128)S(1)} %bitcast.11, f32[96,8,128]{2,1,0:T(8,128)S(1)} %get-tuple-element.32.bred_ref, f32[8,4096]{1,0:T(8,128)S(1)} %get-tuple-element.33.scaled_ref), custom_call_target="tpu_custom_call" | custom-call | tf_op jit(solution)/shard_map/combine/pallas_call | solution.py:495
  (4 shorter events, 0.1 us)
Async XLA Ops:
  0.6 1.0 %copy-start = (f32[8,3,4,8,128]{4,3,2,1,0:T(8,128)S(1)}, f32[8,3,4,8,128]{4,3,2,1,0:T(8,128)}, u32[]{:S(2)}) copy-start(f32[8,3,4,8,128]{4,3,2,1,0:T(8,128)} %param.5) | copy-start | bytes 1179652
  1.6 0.8 copy-start.1
  2.5 22.2 %collective-permute-start = (f32[54,8,128]{2,1,0:T(8,128)S(1)}, f32[54,8,128]{2,1,0:T(8,128)S(1)}, u32[]{:S(2)}, u32[]{:S(2)}) collective-permute-start(f32[54,8,128]{2,1,0:T(8,128)S(1)} %get-tuple-element.20), channel_id=1, source_target_pairs={{0,16},{16,0},{32,48},{48,32},{64,80},{80,64},{96,112},{112,96},{1... | collective-permute-start | bytes 663560 | tf_op jit(solution)/shard_map/ppermute | solution.py:422
  6.6 18.3 %collective-permute-start.1 = (f32[54,8,128]{2,1,0:T(8,128)S(1)}, f32[54,8,128]{2,1,0:T(8,128)S(1)}, u32[]{:S(2)}, u32[]{:S(2)}) collective-permute-start(f32[54,8,128]{2,1,0:T(8,128)S(1)} %get-tuple-element.21), channel_id=1, source_target_pairs={{496,0},{0,496},{16,32},{32,16},{48,64},{64,48},{80,96},{96,80},{1... | collective-permute-start | bytes 663560 | tf_op jit(solution)/shard_map/ppermute | solution.py:421
  21.1 0.8 copy-start.2
  21.8 0.7 copy-start.3
  22.6 0.7 copy-start.4
  25.2 15.6 %collective-permute-start.2 = (f32[4,16,128]{2,1,0:T(8,128)S(1)}, f32[4,16,128]{2,1,0:T(8,128)S(1)}, u32[]{:S(2)}, u32[]{:S(2)}) collective-permute-start(f32[4,16,128]{2,1,0:T(8,128)S(1)} %get-tuple-element.28), channel_id=1, source_target_pairs={{0,1},{1,0},{2,3},{3,2},{4,5},{5,4},{6,7},{7,6},{8,9},{9,8},{10,11... | collective-permute-start | bytes 98312 | tf_op jit(solution)/shard_map/ppermute | solution.py:422
  30.1 10.7 %collective-permute-start.3 = (f32[4,16,128]{2,1,0:T(8,128)S(1)}, f32[4,16,128]{2,1,0:T(8,128)S(1)}, u32[]{:S(2)}, u32[]{:S(2)}) collective-permute-start(f32[4,16,128]{2,1,0:T(8,128)S(1)} %get-tuple-element.29), channel_id=1, source_target_pairs={{15,0},{0,15},{1,2},{2,1},{3,4},{4,3},{5,6},{6,5},{7,8},{8,7},{9,1... | collective-permute-start | bytes 98312 | tf_op jit(solution)/shard_map/ppermute | solution.py:421

commit v5 on v4

--- a/solution.py
+++ b/solution.py
@@ -49,12 +49,10 @@
     return lax.axis_index("core") == 1
 
 
-def pack_rows_kernel(vec_ref, back_ref, all_ref, one_ref, two_ref):
+def pack_rows_kernel(own_ref, one_ref, two_ref):
     odd = odd_row()
-    all_ref[0 : K * PLANES] = vec_ref[...]
-    all_ref[K * PLANES : FIELDS] = back_ref[...]
-    first = all_ref[0:HALF]
-    second = roll(all_ref[HALF:FIELDS], 4, 1)
+    first = own_ref[0:HALF]
+    second = roll(own_ref[HALF:FIELDS], 4, 1)
     top = iota((HALF, ROWS, COLS), 1) < 4
     down = jnp.where(top, first, second)
     up = jnp.where(top, second, first)
@@ -458,12 +456,13 @@
     obs_all = float(OBS * devices_all)
     vec = vectors.reshape(K * PLANES, ROWS, COLS)
     back = background.reshape(PLANES, ROWS, COLS)
-    own, *packed = pl.pallas_call(
+    own = jnp.concatenate([vec, back], axis=0)
+    packed = pl.pallas_call(
         pack_rows_kernel,
-        out_shape=(shape(FIELDS, ROWS, COLS),) + (shape(HALF, ROWS, COLS),) * 2,
+        out_shape=(shape(HALF, ROWS, COLS),) * 2,
         compiler_params=small(8),
         name="pack_rows",
-    )(vec, back)
+    )(own)
     got = swap(packed, GX)
     weights = pl.pallas_call(
         weights_kernel,

time: 84.6 us -> 83.7 us (0.989)
  local copies, waits for them, and re-layouts: 4.01 us -> 2.22 us
  other arithmetic: 0.04 us -> 1.09 us
    unnamed x10 -> x6, local copies, waits for them, and re-layouts: 3.97 us -> 2.19 us
    concatenate x0 -> x1, other arithmetic: none -> 1.06 us  [local(): own = jnp.concatenate([vec, back], axis=0)]
  transfers between devices with their start and end apart: 4 -> 4, of which waited for: 1 -> 1; matrix products, arithmetic and copies ran while one was open for 0% -> 0% of each run, Pallas kernels for 11% -> 12%
where the time goes in v5:
time: 83.7 us; the launch traced here: 83.2 us
  blocking collectives  39.6 us (47%)
  starting transfers between devices  26 us (31%)
  Pallas kernels  13.5 us (16%)
  local copies, waits for them, and re-layouts  2.22 us (3%)
  other arithmetic  1.09 us (1%)
    all_to_all x2, blocking collectives, spread(): return lax.all_to_all(copies, axes, 0, 0, tiled=True).sum(axis=0)  39.6 us
    ppermute x2, starting transfers between devices, swap(): far = lax.ppermute(packed[1], axes, second)  17.1 us
    ppermute x2, starting transfers between devices, swap(): near = lax.ppermute(packed[0], axes, first)  8.89 us
    pallas_call x1, Pallas kernels, local(): pl.pallas_call(inner_kernel, out_shape=(shape(K, COLS, COLS), shape(STRIP...  8.08 us
    pallas_call x1, Pallas kernels, main_call(): pl.pallas_call(main_kernel, out_shape=(shape(K * PLANES, ROWS, COLS), sha...  2.27 us
    unnamed x6, local copies, waits for them, and re-layouts  2.19 us
  transfers between devices with their start and end apart: 4, of which 1 were waited for; matrix products, arithmetic and copies ran while one was open for 0% of the time, Pallas kernels for 12%

profile of v5, /device:TPU:1, one launch (start us, length us, event | category | flops | bytes accessed | tf_op | source)
XLA Modules:
  0.0 83.2 jit_solution(16813026353368808727)
XLA Ops:
  0.6 1.1 %pad_maximum_fusion.own_ref = f32[108,8,128]{2,1,0:T(8,128)S(1)} fusion(f32[12,8,128]{2,1,0:T(8,128)} %bitcast.15, f32[96,8,128]{2,1,0:T(8,128)} %bitcast.13), kind=kLoop, calls=%fused_computation | loop fusion | flops 110592 | bytes 884736 | tf_op jit(solution)/shard_map/concatenate | solution.py:459
  1.7 0.1 pack_rows.1
  1.8 4.0 %collective-permute-start = (f32[54,8,128]{2,1,0:T(8,128)S(1)}, f32[54,8,128]{2,1,0:T(8,128)S(1)}, u32[]{:S(2)}, u32[]{:S(2)}) collective-permute-start(f32[54,8,128]{2,1,0:T(8,128)S(1)} %get-tuple-element.18), channel_id=1, source_target_pairs={{0,16},{16,0},{32,48},{48,32},{64,80},{80,64},{96,112},{112,96},{1... | collective-permute-start | bytes 663560 | tf_op jit(solution)/shard_map/ppermute | solution.py:420
  5.8 14.5 %collective-permute-start.1 = (f32[54,8,128]{2,1,0:T(8,128)S(1)}, f32[54,8,128]{2,1,0:T(8,128)S(1)}, u32[]{:S(2)}, u32[]{:S(2)}) collective-permute-start(f32[54,8,128]{2,1,0:T(8,128)S(1)} %get-tuple-element.19), channel_id=1, source_target_pairs={{496,0},{0,496},{16,32},{32,16},{48,64},{64,48},{80,96},{96,80},{1... | collective-permute-start | bytes 663560 | tf_op jit(solution)/shard_map/ppermute | solution.py:419
  20.3 0.0 copy-start
  20.3 0.7 copy-done
  21.0 0.0 copy-start.1
  21.1 0.7 copy-done.1
  21.8 0.0 copy-start.2
  21.8 0.7 copy-done.2
  22.5 1.5 %weights.1 = (bf16[256,4096]{1,0:T(8,128)(2,1)S(1)}, f32[128,4096]{1,0:T(8,128)S(1)}, f32[8,4096]{1,0:T(8,128)S(1)}) custom-call(s32[1,4096]{1,0:T(1,128)S(1)} %bitcast.11, f32[2,4096]{1,0:T(2,128)S(1)} %copy-done, f32[1,4096]{1,0:T(1,128)S(1)} %bitcast.12), custom_call_target="tpu_custom_call" | custom-call | flops 3000000000 | tf_op jit(solution)/shard_map/weights/pallas_call | solution.py:467
  24.0 0.0 collective-permute-done.got_one
  24.0 0.1 collective-permute-done.1.got_two
  24.1 0.3 pack_cols.1
  24.4 4.9 %collective-permute-start.2 = (f32[4,16,128]{2,1,0:T(8,128)S(1)}, f32[4,16,128]{2,1,0:T(8,128)S(1)}, u32[]{:S(2)}, u32[]{:S(2)}) collective-permute-start(f32[4,16,128]{2,1,0:T(8,128)S(1)} %get-tuple-element.26), channel_id=1, source_target_pairs={{0,1},{1,0},{2,3},{3,2},{4,5},{5,4},{6,7},{7,6},{8,9},{9,8},{10,11... | collective-permute-start | bytes 98312 | tf_op jit(solution)/shard_map/ppermute | solution.py:420
  29.3 2.6 %collective-permute-start.3 = (f32[4,16,128]{2,1,0:T(8,128)S(1)}, f32[4,16,128]{2,1,0:T(8,128)S(1)}, u32[]{:S(2)}, u32[]{:S(2)}) collective-permute-start(f32[4,16,128]{2,1,0:T(8,128)S(1)} %get-tuple-element.27), channel_id=1, source_target_pairs={{15,0},{0,15},{1,2},{2,1},{3,4},{4,3},{5,6},{6,5},{7,8},{8,7},{9,1... | collective-permute-start | bytes 98312 | tf_op jit(solution)/shard_map/ppermute | solution.py:419
  31.9 8.1 %inner.1 = (f32[8,128,128]{2,1,0:T(8,128)S(1)}, f32[28,16,128]{2,1,0:T(8,128)S(1)}, f32[8,4096]{1,0:T(8,128)S(1)}) custom-call(f32[108,16,128]{2,1,0:T(8,128)S(1)} %get-tuple-element.20.ext_ref, bf16[256,4096]{1,0:T(8,128)(2,1)S(1)} %get-tuple-element.21.pick_ref, f32[128,4096]{1,0:T(8,128)S(1)} %get-tuple-element.22.weight_ref), custom_call_target="tpu_custom_call" | custom-call | flops 8000000000 | tf_op jit(solution)/shard_map/inner/pallas_call | solution.py:484
  40.0 0.0 collective-permute-done.2.got_one
  40.0 0.0 collective-permute-done.3.got_two
  40.0 2.3 %edges.1 = (f32[96,8,128]{2,1,0:T(8,128)S(1)}, f32[8,4096]{1,0:T(8,128)S(1)}, f32[1,128]{1,0:T(1,128)S(1)}) custom-call(f32[8,128,128]{2,1,0:T(8,128)S(1)} %get-tuple-element.23.rows_ref, f32[28,16,128]{2,1,0:T(8,128)S(1)} %get-tuple-element.24.strip_ref, f32[8,4096]{1,0:T(8,128)S(1)} %get-tuple-element.25.part_ref, ...), custom_call_target="tpu_custom_call" | custom-call | tf_op jit(solution)/shard_map/edges/pallas_call | solution.py:435
  42.3 22.3 %all_to_all.10 = f32[32,1,128]{2,1,0:T(1,128)S(1)} all-to-all(f32[32,1,128]{2,1,0:T(1,128)S(1)} %broadcast_in_dim.7), channel_id=1, replica_groups=mesh['z_lo'=8,'y'=4,'z_hi'=2,'x'=4,'core'=2] {'y','x','core'}, dimensions={0} | all-to-all | bytes 32768 | tf_op jit(solution)/shard_map/all_to_all | solution.py:431
  64.7 17.3 %all_to_all.11 = f32[16,1,128]{2,1,0:T(1,128)S(1)} all-to-all(f32[16,1,128]{2,1,0:T(1,128)S(1)} %broadcast_in_dim.16), channel_id=1, replica_groups=mesh['z_lo'=8,'y'=4,'z_hi'=2,'x'=4,'core'=2] {'z_lo','z_hi'}, dimensions={0} | all-to-all | bytes 16384 | tf_op jit(solution)/shard_map/all_to_all | solution.py:431
  81.9 1.3 %combine.1 = (f32[96,8,128]{2,1,0:T(8,128)}, f32[8,4096]{1,0:T(8,128)}) custom-call(f32[1,128]{1,0:T(1,128)S(1)} %bitcast.9, f32[96,8,128]{2,1,0:T(8,128)S(1)} %get-tuple-element.30.bred_ref, f32[8,4096]{1,0:T(8,128)S(1)} %get-tuple-element.31.scaled_ref), custom_call_target="tpu_custom_call" | custom-call | tf_op jit(solution)/shard_map/combine/pallas_call | solution.py:494
  (4 shorter events, 0.1 us)
Async XLA Ops:
  1.8 22.2 %collective-permute-start = (f32[54,8,128]{2,1,0:T(8,128)S(1)}, f32[54,8,128]{2,1,0:T(8,128)S(1)}, u32[]{:S(2)}, u32[]{:S(2)}) collective-permute-start(f32[54,8,128]{2,1,0:T(8,128)S(1)} %get-tuple-element.18), channel_id=1, source_target_pairs={{0,16},{16,0},{32,48},{48,32},{64,80},{80,64},{96,112},{112,96},{1... | collective-permute-start | bytes 663560 | tf_op jit(solution)/shard_map/ppermute | solution.py:420
  5.8 18.3 %collective-permute-start.1 = (f32[54,8,128]{2,1,0:T(8,128)S(1)}, f32[54,8,128]{2,1,0:T(8,128)S(1)}, u32[]{:S(2)}, u32[]{:S(2)}) collective-permute-start(f32[54,8,128]{2,1,0:T(8,128)S(1)} %get-tuple-element.19), channel_id=1, source_target_pairs={{496,0},{0,496},{16,32},{32,16},{48,64},{64,48},{80,96},{96,80},{1... | collective-permute-start | bytes 663560 | tf_op jit(solution)/shard_map/ppermute | solution.py:419
  20.3 0.8 copy-start
  21.0 0.7 copy-start.1
  21.8 0.7 copy-start.2
  24.4 15.6 %collective-permute-start.2 = (f32[4,16,128]{2,1,0:T(8,128)S(1)}, f32[4,16,128]{2,1,0:T(8,128)S(1)}, u32[]{:S(2)}, u32[]{:S(2)}) collective-permute-start(f32[4,16,128]{2,1,0:T(8,128)S(1)} %get-tuple-element.26), channel_id=1, source_target_pairs={{0,1},{1,0},{2,3},{3,2},{4,5},{5,4},{6,7},{7,6},{8,9},{9,8},{10,11... | collective-permute-start | bytes 98312 | tf_op jit(solution)/shard_map/ppermute | solution.py:420
  29.3 10.7 %collective-permute-start.3 = (f32[4,16,128]{2,1,0:T(8,128)S(1)}, f32[4,16,128]{2,1,0:T(8,128)S(1)}, u32[]{:S(2)}, u32[]{:S(2)}) collective-permute-start(f32[4,16,128]{2,1,0:T(8,128)S(1)} %get-tuple-element.27), channel_id=1, source_target_pairs={{15,0},{0,15},{1,2},{2,1},{3,4},{4,3},{5,6},{6,5},{7,8},{8,7},{9,1... | collective-permute-start | bytes 98312 | tf_op jit(solution)/shard_map/ppermute | solution.py:419

commit v6 on v5

--- a/solution.py
+++ b/solution.py
@@ -123,15 +123,19 @@
     ref[k, OWN + PLANES + plane : OWN + PLANES + plane + 1] = field[ROWS : ROWS + 1]
 
 
+def put_strips(strip_ref, tile_of):
+    lane = iota((ROWS, COLS), 1)
+    for t in range(STRIPS):
+        strip = jnp.zeros((ROWS, COLS), F32)
+        for kk, field in enumerate(strip_fields(t)):
+            tile = tile_of(field)
+            strip = jnp.where(lane >= 32 * kk + 4, roll(tile, 32 * kk + 4, 1), strip)
+            strip = jnp.where(lane >= 32 * kk + 16, roll(tile, 32 * kk + 28, 1), strip)
+        strip_ref[t] = strip
+
+
 def inner_kernel(ext_ref, pick_ref, weight_ref, rows_ref, strip_ref, part_ref, table_ref):
-    lane = iota((2 * ROWS, COLS), 1)
-    for t in range(STRIPS):
-        strip = jnp.zeros((2 * ROWS, COLS), F32)
-        for kk, field in enumerate(strip_fields(t)):
-            plane = ext_ref[field]
-            strip = jnp.where(lane >= 32 * kk + 4, roll(plane, 32 * kk + 4, 1), strip)
-            strip = jnp.where(lane >= 32 * kk + 16, roll(plane, 32 * kk + 28, 1), strip)
-        strip_ref[t] = strip
+    put_strips(strip_ref, lambda field: ext_ref[field, ROWS : 2 * ROWS])
     rows_ref[:, OWN + 2 * PLANES :] = jnp.zeros((K, COLS - OWN - 2 * PLANES, COLS), F32)
     for level in range(L):
         base = K * PLANES + level
@@ -150,7 +154,7 @@
                     put_rows(rows_ref, i * BATCH + b, c * L + level, done[c][b])
             return carry
 
-        lax.fori_loop(0, K // BATCH, body, 0)
+        lax.fori_loop(0, K // BATCH, body, 0, unroll=True)
     inner = iota((COLS, COLS), 1)
     inner = (inner >= 3) & (inner < COLS - 3)
     for k in range(K):
@@ -189,7 +193,11 @@
     ref[at : at + value.shape[0], COLS : 2 * COLS] = low
 
 
-def weights_kernel(site_ref, off_ref, err_ref, pick_ref, weight_ref, ends_ref):
+def weights_kernel(
+    site_ref, off_ref, err_ref, own_ref, pick_ref, weight_ref, ends_ref, strip_ref
+):
+    put_strips(strip_ref, lambda field: own_ref[field])
+
     def step(i, carry):
         at = pl.ds(pl.multiple_of(i * CHUNK, CHUNK), CHUNK)
         site = site_ref[:, at]
@@ -235,7 +243,7 @@
 
 
 def main_kernel(
-    rows_ref, strip_ref, part_ref, got_one, got_two, pick_ref, ends_ref,
+    own_ref, rows_ref, strip_ref, part_ref, got_one, got_two, pick_ref, ends_ref,
     bred_ref, scaled_ref, sums_ref,
     whole_ref, side_ref, edge_ref, pair_ref,
 ):
@@ -249,7 +257,8 @@
             t = group * 8 + u
             if t >= STRIPS:
                 break
-            strip = jnp.where(eighth == 0, roll(left, 4 - 4 * u, 1), strip_ref[t])
+            strip = jnp.concatenate([own_ref[t], strip_ref[t]], axis=0)
+            strip = jnp.where(eighth == 0, roll(left, 4 - 4 * u, 1), strip)
             whole_ref[t] = jnp.where(eighth == 7, roll(right, 28 - 4 * u, 1), strip)
     side_ref[:, OWN + 2 * PLANES :] = jnp.zeros((2, COLS - OWN - 2 * PLANES, COLS), F32)
     results = []
@@ -467,12 +476,14 @@
     weights = pl.pallas_call(
         weights_kernel,
         out_shape=(
-            jax.ShapeDtypeStruct((2 * COLS, OBS), jnp.bfloat16), shape(COLS, OBS), shape(ROWS, OBS)
+            jax.ShapeDtypeStruct((2 * COLS, OBS), jnp.bfloat16),
+            shape(COLS, OBS), shape(ROWS, OBS),
+            shape(STRIPS, ROWS, COLS),
         ),
         compiler_params=small(8),
         cost_estimate=busy(3),
         name="weights",
-    )(obs_site.reshape(1, OBS), obs_offset, obs_error.reshape(1, OBS))
+    )(obs_site.reshape(1, OBS), obs_offset, obs_error.reshape(1, OBS), own)
     ext, *packed = pl.pallas_call(
         pack_cols_kernel,
         out_shape=(shape(FIELDS, 2 * ROWS, COLS),) + (shape(GROUPS, 2 * ROWS, COLS),) * 2,
@@ -480,16 +491,16 @@
         name="pack_cols",
     )(own, *got)
     got = swap(packed, GY)
-    pick, weight, ends = weights
+    pick, weight, ends, own_strips = weights
     mine = pl.pallas_call(
         inner_kernel,
-        out_shape=(shape(K, COLS, COLS), shape(STRIPS, 2 * ROWS, COLS), shape(K, OBS)),
+        out_shape=(shape(K, COLS, COLS), shape(STRIPS, ROWS, COLS), shape(K, OBS)),
         scratch_shapes=[pltpu.VMEM((K * COLS, 2 * COLS), jnp.bfloat16)],
         compiler_params=small(16),
         cost_estimate=busy(8),
         name="inner",
     )(ext, pick, weight)
-    bred, scaled, sums = main_call(*mine, *got, pick, ends)
+    bred, scaled, sums = main_call(own_strips, *mine, *got, pick, ends)
     sums = spread(spread(sums, FLAT), DEEP)
     analysis, perturb = pl.pallas_call(
         functools.partial(final_kernel, cells_all, obs_all),

time: 83.7 us -> 83.7 us (level)
  blocking collectives: 39.6 us -> 41.2 us
  Pallas kernels: 13.5 us -> 12.1 us
    pallas_call x1, Pallas kernels: 8.08 us -> 6.4 us  [local(): pl.pallas_call(inner_kernel, out_shape=(shape(K, COLS, COLS), shape(STRIP...]
    all_to_all x2, blocking collectives: 39.6 us -> 41.2 us  [spread(): return lax.all_to_all(copies, axes, 0, 0, tiled=True).sum(axis=0)]
  transfers between devices with their start and end apart: 4 -> 4, of which waited for: 1 -> 0; matrix products, arithmetic and copies ran while one was open for 0% -> 0% of each run, Pallas kernels for 12% -> 10%
where the time goes in v6:
time: 83.7 us; the launch traced here: 83.2 us
  blocking collectives  41.2 us (49%)
  starting transfers between devices  25.8 us (31%)
  Pallas kernels  12.1 us (14%)
  local copies, waits for them, and re-layouts  2.22 us (3%)
  other arithmetic  1.09 us (1%)
    all_to_all x2, blocking collectives, spread(): return lax.all_to_all(copies, axes, 0, 0, tiled=True).sum(axis=0)  41.2 us
    ppermute x2, starting transfers between devices, swap(): far = lax.ppermute(packed[1], axes, second)  17.1 us
    ppermute x2, starting transfers between devices, swap(): near = lax.ppermute(packed[0], axes, first)  8.68 us
    pallas_call x1, Pallas kernels, local(): pl.pallas_call(inner_kernel, out_shape=(shape(K, COLS, COLS), shape(STRIP...  6.4 us
    pallas_call x1, Pallas kernels, main_call(): pl.pallas_call(main_kernel, out_shape=(shape(K * PLANES, ROWS, COLS), sha...  2.27 us
    unnamed x6, local copies, waits for them, and re-layouts  2.19 us
    pallas_call x1, Pallas kernels, local(): pl.pallas_call(weights_kernel, out_shape=(jax.ShapeDtypeStruct((2 * COLS,...  1.79 us
  transfers between devices with their start and end apart: 4, of which 0 were waited for; matrix products, arithmetic and copies ran while one was open for 0% of the time, Pallas kernels for 10%

profile of v6, /device:TPU:1, one launch (start us, length us, event | category | flops | bytes accessed | tf_op | source)
XLA Modules:
  0.0 83.2 jit_solution(224321311715986697)
XLA Ops:
  0.6 1.1 %pad_maximum_fusion.own_ref = f32[108,8,128]{2,1,0:T(8,128)S(1)} fusion(f32[12,8,128]{2,1,0:T(8,128)} %bitcast.15, f32[96,8,128]{2,1,0:T(8,128)} %bitcast.13), kind=kLoop, calls=%fused_computation | loop fusion | flops 110592 | bytes 884736 | tf_op jit(solution)/shard_map/concatenate | solution.py:468
  1.7 0.1 pack_rows.1
  1.8 4.0 %collective-permute-start = (f32[54,8,128]{2,1,0:T(8,128)S(1)}, f32[54,8,128]{2,1,0:T(8,128)S(1)}, u32[]{:S(2)}, u32[]{:S(2)}) collective-permute-start(f32[54,8,128]{2,1,0:T(8,128)S(1)} %get-tuple-element.20), channel_id=1, source_target_pairs={{0,16},{16,0},{32,48},{48,32},{64,80},{80,64},{96,112},{112,96},{1... | collective-permute-start | bytes 663560 | tf_op jit(solution)/shard_map/ppermute | solution.py:429
  5.8 14.5 %collective-permute-start.1 = (f32[54,8,128]{2,1,0:T(8,128)S(1)}, f32[54,8,128]{2,1,0:T(8,128)S(1)}, u32[]{:S(2)}, u32[]{:S(2)}) collective-permute-start(f32[54,8,128]{2,1,0:T(8,128)S(1)} %get-tuple-element.21), channel_id=1, source_target_pairs={{496,0},{0,496},{16,32},{32,16},{48,64},{64,48},{80,96},{96,80},{1... | collective-permute-start | bytes 663560 | tf_op jit(solution)/shard_map/ppermute | solution.py:428
  20.3 0.0 copy-start
  20.3 0.7 copy-done
  21.0 0.0 copy-start.1
  21.1 0.7 copy-done.1
  21.8 0.0 copy-start.2
  21.8 0.7 copy-done.2
  22.5 1.8 %weights.1 = (bf16[256,4096]{1,0:T(8,128)(2,1)S(1)}, f32[128,4096]{1,0:T(8,128)S(1)}, f32[8,4096]{1,0:T(8,128)S(1)}, f32[28,8,128]{2,1,0:T(8,128)S(1)}) custom-call(s32[1,4096]{1,0:T(1,128)S(1)} %bitcast.11, f32[2,4096]{1,0:T(2,128)S(1)} %copy-done, f32[1,4096]{1,0:T(1,128)S(1)} %bitcast.12, f32[108,8,128]{2,1,0:T(8,128)S(1)} %pad_maximum_fusion.own_ref), custom_call_target="tpu_custom_call" | custom-call | flops 3000000000 | tf_op jit(solution)/shard_map/weights/pallas_call | solution.py:476
  24.3 0.0 collective-permute-done.got_one
  24.3 0.0 collective-permute-done.1.got_two
  24.3 0.3 pack_cols.1
  24.6 4.7 %collective-permute-start.2 = (f32[4,16,128]{2,1,0:T(8,128)S(1)}, f32[4,16,128]{2,1,0:T(8,128)S(1)}, u32[]{:S(2)}, u32[]{:S(2)}) collective-permute-start(f32[4,16,128]{2,1,0:T(8,128)S(1)} %get-tuple-element.28), channel_id=1, source_target_pairs={{0,1},{1,0},{2,3},{3,2},{4,5},{5,4},{6,7},{7,6},{8,9},{9,8},{10,11... | collective-permute-start | bytes 98312 | tf_op jit(solution)/shard_map/ppermute | solution.py:429
  29.3 2.6 %collective-permute-start.3 = (f32[4,16,128]{2,1,0:T(8,128)S(1)}, f32[4,16,128]{2,1,0:T(8,128)S(1)}, u32[]{:S(2)}, u32[]{:S(2)}) collective-permute-start(f32[4,16,128]{2,1,0:T(8,128)S(1)} %get-tuple-element.29), channel_id=1, source_target_pairs={{15,0},{0,15},{1,2},{2,1},{3,4},{4,3},{5,6},{6,5},{7,8},{8,7},{9,1... | collective-permute-start | bytes 98312 | tf_op jit(solution)/shard_map/ppermute | solution.py:428
  31.9 6.4 %inner.1 = (f32[8,128,128]{2,1,0:T(8,128)S(1)}, f32[28,8,128]{2,1,0:T(8,128)S(1)}, f32[8,4096]{1,0:T(8,128)S(1)}) custom-call(f32[108,16,128]{2,1,0:T(8,128)S(1)} %get-tuple-element.22.ext_ref, bf16[256,4096]{1,0:T(8,128)(2,1)S(1)} %get-tuple-element.23.pick_ref, f32[128,4096]{1,0:T(8,128)S(1)} %get-tuple-element.24.weight_ref), custom_call_target="tpu_custom_call" | custom-call | flops 8000000000 | tf_op jit(solution)/shard_map/inner/pallas_call | solution.py:495
  38.3 0.0 collective-permute-done.2.got_one
  38.3 0.0 collective-permute-done.3.got_two
  38.3 2.3 %edges.1 = (f32[96,8,128]{2,1,0:T(8,128)S(1)}, f32[8,4096]{1,0:T(8,128)S(1)}, f32[1,128]{1,0:T(1,128)S(1)}) custom-call(f32[28,8,128]{2,1,0:T(8,128)S(1)} %get-tuple-element.19.own_ref, f32[8,128,128]{2,1,0:T(8,128)S(1)} %get-tuple-element.25.rows_ref, f32[28,8,128]{2,1,0:T(8,128)S(1)} %get-tuple-element.26.strip_ref, ...), custom_call_target="tpu_custom_call" | custom-call | tf_op jit(solution)/shard_map/edges/pallas_call | solution.py:444
  40.7 22.3 %all_to_all.10 = f32[32,1,128]{2,1,0:T(1,128)S(1)} all-to-all(f32[32,1,128]{2,1,0:T(1,128)S(1)} %broadcast_in_dim.7), channel_id=1, replica_groups=mesh['z_lo'=8,'y'=4,'z_hi'=2,'x'=4,'core'=2] {'y','x','core'}, dimensions={0} | all-to-all | bytes 32768 | tf_op jit(solution)/shard_map/all_to_all | solution.py:440
  63.0 19.0 %all_to_all.11 = f32[16,1,128]{2,1,0:T(1,128)S(1)} all-to-all(f32[16,1,128]{2,1,0:T(1,128)S(1)} %broadcast_in_dim.16), channel_id=1, replica_groups=mesh['z_lo'=8,'y'=4,'z_hi'=2,'x'=4,'core'=2] {'z_lo','z_hi'}, dimensions={0} | all-to-all | bytes 16384 | tf_op jit(solution)/shard_map/all_to_all | solution.py:440
  82.0 1.3 %combine.1 = (f32[96,8,128]{2,1,0:T(8,128)}, f32[8,4096]{1,0:T(8,128)}) custom-call(f32[1,128]{1,0:T(1,128)S(1)} %bitcast.9, f32[96,8,128]{2,1,0:T(8,128)S(1)} %get-tuple-element.32.bred_ref, f32[8,4096]{1,0:T(8,128)S(1)} %get-tuple-element.33.scaled_ref), custom_call_target="tpu_custom_call" | custom-call | tf_op jit(solution)/shard_map/combine/pallas_call | solution.py:505
  (4 shorter events, 0.1 us)
Async XLA Ops:
  1.8 22.5 %collective-permute-start = (f32[54,8,128]{2,1,0:T(8,128)S(1)}, f32[54,8,128]{2,1,0:T(8,128)S(1)}, u32[]{:S(2)}, u32[]{:S(2)}) collective-permute-start(f32[54,8,128]{2,1,0:T(8,128)S(1)} %get-tuple-element.20), channel_id=1, source_target_pairs={{0,16},{16,0},{32,48},{48,32},{64,80},{80,64},{96,112},{112,96},{1... | collective-permute-start | bytes 663560 | tf_op jit(solution)/shard_map/ppermute | solution.py:429
  5.8 18.5 %collective-permute-start.1 = (f32[54,8,128]{2,1,0:T(8,128)S(1)}, f32[54,8,128]{2,1,0:T(8,128)S(1)}, u32[]{:S(2)}, u32[]{:S(2)}) collective-permute-start(f32[54,8,128]{2,1,0:T(8,128)S(1)} %get-tuple-element.21), channel_id=1, source_target_pairs={{496,0},{0,496},{16,32},{32,16},{48,64},{64,48},{80,96},{96,80},{1... | collective-permute-start | bytes 663560 | tf_op jit(solution)/shard_map/ppermute | solution.py:428
  20.3 0.8 copy-start
  21.0 0.7 copy-start.1
  21.8 0.7 copy-start.2
  24.6 13.7 %collective-permute-start.2 = (f32[4,16,128]{2,1,0:T(8,128)S(1)}, f32[4,16,128]{2,1,0:T(8,128)S(1)}, u32[]{:S(2)}, u32[]{:S(2)}) collective-permute-start(f32[4,16,128]{2,1,0:T(8,128)S(1)} %get-tuple-element.28), channel_id=1, source_target_pairs={{0,1},{1,0},{2,3},{3,2},{4,5},{5,4},{6,7},{7,6},{8,9},{9,8},{10,11... | collective-permute-start | bytes 98312 | tf_op jit(solution)/shard_map/ppermute | solution.py:429
  29.3 9.0 %collective-permute-start.3 = (f32[4,16,128]{2,1,0:T(8,128)S(1)}, f32[4,16,128]{2,1,0:T(8,128)S(1)}, u32[]{:S(2)}, u32[]{:S(2)}) collective-permute-start(f32[4,16,128]{2,1,0:T(8,128)S(1)} %get-tuple-element.29), channel_id=1, source_target_pairs={{15,0},{0,15},{1,2},{2,1},{3,4},{4,3},{5,6},{6,5},{7,8},{8,7},{9,1... | collective-permute-start | bytes 98312 | tf_op jit(solution)/shard_map/ppermute | solution.py:428

commit v7 on v6

--- a/solution.py
+++ b/solution.py
@@ -345,8 +345,8 @@
         total = a[j][j]
         for k in range(j):
             total = total - low[j][k] * low[j][k]
-        root = jnp.sqrt(total)
-        inv[j][j] = 1.0 / root
+        guess = lax.rsqrt(total)
+        inv[j][j] = guess * (1.5 - 0.5 * (total * guess) * guess)
         for i in range(j + 1, n):
             total = a[i][j]
             for k in range(j):
@@ -501,7 +501,7 @@
         name="inner",
     )(ext, pick, weight)
     bred, scaled, sums = main_call(own_strips, *mine, *got, pick, ends)
-    sums = spread(spread(sums, FLAT), DEEP)
+    sums = spread(spread(sums, DEEP), FLAT)
     analysis, perturb = pl.pallas_call(
         functools.partial(final_kernel, cells_all, obs_all),
         out_shape=(shape(K * PLANES, ROWS, COLS), shape(K, OBS)),

time: 83.7 us -> 83.7 us (level)
  no operation moved by 1% of the time
where the time goes in v7:
time: 83.7 us; the launch traced here: 83.3 us
  blocking collectives  41.3 us (49%)
  starting transfers between devices  25.8 us (31%)
  Pallas kernels  12.1 us (14%)
  local copies, waits for them, and re-layouts  2.22 us (3%)
  other arithmetic  1.09 us (1%)
    all_to_all x2, blocking collectives, spread(): return lax.all_to_all(copies, axes, 0, 0, tiled=True).sum(axis=0)  41.3 us
    ppermute x2, starting transfers between devices, swap(): far = lax.ppermute(packed[1], axes, second)  17.1 us
    ppermute x2, starting transfers between devices, swap(): near = lax.ppermute(packed[0], axes, first)  8.68 us
    pallas_call x1, Pallas kernels, local(): pl.pallas_call(inner_kernel, out_shape=(shape(K, COLS, COLS), shape(STRIP...  6.4 us
    pallas_call x1, Pallas kernels, main_call(): pl.pallas_call(main_kernel, out_shape=(shape(K * PLANES, ROWS, COLS), sha...  2.27 us
    unnamed x6, local copies, waits for them, and re-layouts  2.19 us
    pallas_call x1, Pallas kernels, local(): pl.pallas_call(weights_kernel, out_shape=(jax.ShapeDtypeStruct((2 * COLS,...  1.79 us
  transfers between devices with their start and end apart: 4, of which 0 were waited for; matrix products, arithmetic and copies ran while one was open for 0% of the time, Pallas kernels for 10%

profile of v7, /device:TPU:1, one launch (start us, length us, event | category | flops | bytes accessed | tf_op | source)
XLA Modules:
  0.0 83.3 jit_solution(5862436224218448011)
XLA Ops:
  0.6 1.1 %pad_maximum_fusion.own_ref = f32[108,8,128]{2,1,0:T(8,128)S(1)} fusion(f32[12,8,128]{2,1,0:T(8,128)} %bitcast.15, f32[96,8,128]{2,1,0:T(8,128)} %bitcast.13), kind=kLoop, calls=%fused_computation | loop fusion | flops 110592 | bytes 884736 | tf_op jit(solution)/shard_map/concatenate | solution.py:468
  1.7 0.1 pack_rows.1
  1.8 4.0 %collective-permute-start = (f32[54,8,128]{2,1,0:T(8,128)S(1)}, f32[54,8,128]{2,1,0:T(8,128)S(1)}, u32[]{:S(2)}, u32[]{:S(2)}) collective-permute-start(f32[54,8,128]{2,1,0:T(8,128)S(1)} %get-tuple-element.20), channel_id=1, source_target_pairs={{0,16},{16,0},{32,48},{48,32},{64,80},{80,64},{96,112},{112,96},{1... | collective-permute-start | bytes 663560 | tf_op jit(solution)/shard_map/ppermute | solution.py:429
  5.8 14.5 %collective-permute-start.1 = (f32[54,8,128]{2,1,0:T(8,128)S(1)}, f32[54,8,128]{2,1,0:T(8,128)S(1)}, u32[]{:S(2)}, u32[]{:S(2)}) collective-permute-start(f32[54,8,128]{2,1,0:T(8,128)S(1)} %get-tuple-element.21), channel_id=1, source_target_pairs={{496,0},{0,496},{16,32},{32,16},{48,64},{64,48},{80,96},{96,80},{1... | collective-permute-start | bytes 663560 | tf_op jit(solution)/shard_map/ppermute | solution.py:428
  20.3 0.0 copy-start
  20.3 0.7 copy-done
  21.0 0.0 copy-start.1
  21.1 0.7 copy-done.1
  21.8 0.0 copy-start.2
  21.8 0.7 copy-done.2
  22.5 1.8 %weights.1 = (bf16[256,4096]{1,0:T(8,128)(2,1)S(1)}, f32[128,4096]{1,0:T(8,128)S(1)}, f32[8,4096]{1,0:T(8,128)S(1)}, f32[28,8,128]{2,1,0:T(8,128)S(1)}) custom-call(s32[1,4096]{1,0:T(1,128)S(1)} %bitcast.11, f32[2,4096]{1,0:T(2,128)S(1)} %copy-done, f32[1,4096]{1,0:T(1,128)S(1)} %bitcast.12, f32[108,8,128]{2,1,0:T(8,128)S(1)} %pad_maximum_fusion.own_ref), custom_call_target="tpu_custom_call" | custom-call | flops 3000000000 | tf_op jit(solution)/shard_map/weights/pallas_call | solution.py:476
  24.3 0.0 collective-permute-done.got_one
  24.3 0.0 collective-permute-done.1.got_two
  24.3 0.3 pack_cols.1
  24.6 4.7 %collective-permute-start.2 = (f32[4,16,128]{2,1,0:T(8,128)S(1)}, f32[4,16,128]{2,1,0:T(8,128)S(1)}, u32[]{:S(2)}, u32[]{:S(2)}) collective-permute-start(f32[4,16,128]{2,1,0:T(8,128)S(1)} %get-tuple-element.28), channel_id=1, source_target_pairs={{0,1},{1,0},{2,3},{3,2},{4,5},{5,4},{6,7},{7,6},{8,9},{9,8},{10,11... | collective-permute-start | bytes 98312 | tf_op jit(solution)/shard_map/ppermute | solution.py:429
  29.3 2.6 %collective-permute-start.3 = (f32[4,16,128]{2,1,0:T(8,128)S(1)}, f32[4,16,128]{2,1,0:T(8,128)S(1)}, u32[]{:S(2)}, u32[]{:S(2)}) collective-permute-start(f32[4,16,128]{2,1,0:T(8,128)S(1)} %get-tuple-element.29), channel_id=1, source_target_pairs={{15,0},{0,15},{1,2},{2,1},{3,4},{4,3},{5,6},{6,5},{7,8},{8,7},{9,1... | collective-permute-start | bytes 98312 | tf_op jit(solution)/shard_map/ppermute | solution.py:428
  31.9 6.4 %inner.1 = (f32[8,128,128]{2,1,0:T(8,128)S(1)}, f32[28,8,128]{2,1,0:T(8,128)S(1)}, f32[8,4096]{1,0:T(8,128)S(1)}) custom-call(f32[108,16,128]{2,1,0:T(8,128)S(1)} %get-tuple-element.22.ext_ref, bf16[256,4096]{1,0:T(8,128)(2,1)S(1)} %get-tuple-element.23.pick_ref, f32[128,4096]{1,0:T(8,128)S(1)} %get-tuple-element.24.weight_ref), custom_call_target="tpu_custom_call" | custom-call | flops 8000000000 | tf_op jit(solution)/shard_map/inner/pallas_call | solution.py:495
  38.3 0.0 collective-permute-done.2.got_one
  38.3 0.0 collective-permute-done.3.got_two
  38.3 2.3 %edges.1 = (f32[96,8,128]{2,1,0:T(8,128)S(1)}, f32[8,4096]{1,0:T(8,128)S(1)}, f32[1,128]{1,0:T(1,128)S(1)}) custom-call(f32[28,8,128]{2,1,0:T(8,128)S(1)} %get-tuple-element.19.own_ref, f32[8,128,128]{2,1,0:T(8,128)S(1)} %get-tuple-element.25.rows_ref, f32[28,8,128]{2,1,0:T(8,128)S(1)} %get-tuple-element.26.strip_ref, ...), custom_call_target="tpu_custom_call" | custom-call | tf_op jit(solution)/shard_map/edges/pallas_call | solution.py:444
  40.6 23.6 %all_to_all.10 = f32[16,1,128]{2,1,0:T(1,128)S(1)} all-to-all(f32[16,1,128]{2,1,0:T(1,128)S(1)} %broadcast_in_dim.7), channel_id=1, replica_groups=mesh['z_lo'=8,'y'=4,'z_hi'=2,'x'=4,'core'=2] {'z_lo','z_hi'}, dimensions={0} | all-to-all | bytes 16384 | tf_op jit(solution)/shard_map/all_to_all | solution.py:440
  64.3 17.7 %all_to_all.11 = f32[32,1,128]{2,1,0:T(1,128)S(1)} all-to-all(f32[32,1,128]{2,1,0:T(1,128)S(1)} %broadcast_in_dim.16), channel_id=1, replica_groups=mesh['z_lo'=8,'y'=4,'z_hi'=2,'x'=4,'core'=2] {'y','x','core'}, dimensions={0} | all-to-all | bytes 32768 | tf_op jit(solution)/shard_map/all_to_all | solution.py:440
  82.0 1.2 %combine.1 = (f32[96,8,128]{2,1,0:T(8,128)}, f32[8,4096]{1,0:T(8,128)}) custom-call(f32[1,128]{1,0:T(1,128)S(1)} %bitcast.9, f32[96,8,128]{2,1,0:T(8,128)S(1)} %get-tuple-element.32.bred_ref, f32[8,4096]{1,0:T(8,128)S(1)} %get-tuple-element.33.scaled_ref), custom_call_target="tpu_custom_call" | custom-call | tf_op jit(solution)/shard_map/combine/pallas_call | solution.py:505
  (4 shorter events, 0.1 us)
Async XLA Ops:
  1.8 22.5 %collective-permute-start = (f32[54,8,128]{2,1,0:T(8,128)S(1)}, f32[54,8,128]{2,1,0:T(8,128)S(1)}, u32[]{:S(2)}, u32[]{:S(2)}) collective-permute-start(f32[54,8,128]{2,1,0:T(8,128)S(1)} %get-tuple-element.20), channel_id=1, source_target_pairs={{0,16},{16,0},{32,48},{48,32},{64,80},{80,64},{96,112},{112,96},{1... | collective-permute-start | bytes 663560 | tf_op jit(solution)/shard_map/ppermute | solution.py:429
  5.8 18.5 %collective-permute-start.1 = (f32[54,8,128]{2,1,0:T(8,128)S(1)}, f32[54,8,128]{2,1,0:T(8,128)S(1)}, u32[]{:S(2)}, u32[]{:S(2)}) collective-permute-start(f32[54,8,128]{2,1,0:T(8,128)S(1)} %get-tuple-element.21), channel_id=1, source_target_pairs={{496,0},{0,496},{16,32},{32,16},{48,64},{64,48},{80,96},{96,80},{1... | collective-permute-start | bytes 663560 | tf_op jit(solution)/shard_map/ppermute | solution.py:428
  20.3 0.8 copy-start
  21.0 0.7 copy-start.1
  21.8 0.7 copy-start.2
  24.6 13.7 %collective-permute-start.2 = (f32[4,16,128]{2,1,0:T(8,128)S(1)}, f32[4,16,128]{2,1,0:T(8,128)S(1)}, u32[]{:S(2)}, u32[]{:S(2)}) collective-permute-start(f32[4,16,128]{2,1,0:T(8,128)S(1)} %get-tuple-element.28), channel_id=1, source_target_pairs={{0,1},{1,0},{2,3},{3,2},{4,5},{5,4},{6,7},{7,6},{8,9},{9,8},{10,11... | collective-permute-start | bytes 98312 | tf_op jit(solution)/shard_map/ppermute | solution.py:429
  29.3 9.0 %collective-permute-start.3 = (f32[4,16,128]{2,1,0:T(8,128)S(1)}, f32[4,16,128]{2,1,0:T(8,128)S(1)}, u32[]{:S(2)}, u32[]{:S(2)}) collective-permute-start(f32[4,16,128]{2,1,0:T(8,128)S(1)} %get-tuple-element.29), channel_id=1, source_target_pairs={{15,0},{0,15},{1,2},{2,1},{3,4},{4,3},{5,6},{6,5},{7,8},{8,7},{9,1... | collective-permute-start | bytes 98312 | tf_op jit(solution)/shard_map/ppermute | solution.py:428

commit v8 on v6

--- a/solution.py
+++ b/solution.py
@@ -78,8 +78,26 @@
                 moved = roll(ext_ref[field], 32 * kk + 4 * u, 1)
                 down = jnp.where(lane // 4 == 8 * kk + u, moved, down)
                 up = jnp.where(lane // 4 == (8 * kk + u + 31) % 32, moved, up)
-        one_ref[group] = jnp.where(at_odd_col, down, up)
-        two_ref[group] = jnp.where(at_odd_col, up, down)
+        one, two = jnp.where(at_odd_col, down, up), jnp.where(at_odd_col, up, down)
+        at = 2 * group
+        if group < GROUPS - 1:
+            for ref, tile in ((one_ref, one), (two_ref, two)):
+                ref[at] = tile[:ROWS]
+                ref[at + 1] = tile[ROWS:]
+        else:
+            eighth = (iota((ROWS, COLS), 1) & 31) // 4
+            below = eighth < 4
+            above = (eighth < 3) | (eighth == 7)
+            down = jnp.where(below, down[:ROWS], roll(down[ROWS:], 16, 1))
+            up = jnp.where(above, up[:ROWS], roll(up[ROWS:], 16, 1))
+            one_ref[at] = jnp.where(at_odd_col, down, up)
+            two_ref[at] = jnp.where(at_odd_col, up, down)
+
+
+def received(ref, group):
+    first = ref[2 * group]
+    second = ref[2 * group + 1] if group < GROUPS - 1 else roll(first, -16, 1)
+    return jnp.concatenate([first, second], axis=0)
 
 
 def strip_fields(t):
@@ -251,8 +269,9 @@
     lane = iota((2 * ROWS, COLS), 1)
     eighth = (lane & 31) // 4
     for group in range(GROUPS):
-        left = jnp.where(at_odd_col, got_one[group], got_two[group])
-        right = jnp.where(at_odd_col, got_two[group], got_one[group])
+        one, two = received(got_one, group), received(got_two, group)
+        left = jnp.where(at_odd_col, one, two)
+        right = jnp.where(at_odd_col, two, one)
         for u in range(8):
             t = group * 8 + u
             if t >= STRIPS:
@@ -486,7 +505,7 @@
     )(obs_site.reshape(1, OBS), obs_offset, obs_error.reshape(1, OBS), own)
     ext, *packed = pl.pallas_call(
         pack_cols_kernel,
-        out_shape=(shape(FIELDS, 2 * ROWS, COLS),) + (shape(GROUPS, 2 * ROWS, COLS),) * 2,
+        out_shape=(shape(FIELDS, 2 * ROWS, COLS),) + (shape(2 * GROUPS - 1, ROWS, COLS),) * 2,
         compiler_params=small(8),
         name="pack_cols",
     )(own, *got)

time: 83.7 us -> 83.7 us (level)
  no operation moved by 1% of the time
where the time goes in v8:
time: 83.7 us; the launch traced here: 83.2 us
  blocking collectives  41.2 us (49%)
  starting transfers between devices  25.8 us (31%)
  Pallas kernels  12.1 us (14%)
  local copies, waits for them, and re-layouts  2.22 us (3%)
  other arithmetic  1.09 us (1%)
    all_to_all x2, blocking collectives, spread(): return lax.all_to_all(copies, axes, 0, 0, tiled=True).sum(axis=0)  41.2 us
    ppermute x2, starting transfers between devices, swap(): far = lax.ppermute(packed[1], axes, second)  17.1 us
    ppermute x2, starting transfers between devices, swap(): near = lax.ppermute(packed[0], axes, first)  8.68 us
    pallas_call x1, Pallas kernels, local(): pl.pallas_call(inner_kernel, out_shape=(shape(K, COLS, COLS), shape(STRIP...  6.4 us
    pallas_call x1, Pallas kernels, main_call(): pl.pallas_call(main_kernel, out_shape=(shape(K * PLANES, ROWS, COLS), sha...  2.27 us
    unnamed x6, local copies, waits for them, and re-layouts  2.19 us
    pallas_call x1, Pallas kernels, local(): pl.pallas_call(weights_kernel, out_shape=(jax.ShapeDtypeStruct((2 * COLS,...  1.79 us
  transfers between devices with their start and end apart: 4, of which 0 were waited for; matrix products, arithmetic and copies ran while one was open for 0% of the time, Pallas kernels for 10%

profile of v8, /device:TPU:1, one launch (start us, length us, event | category | flops | bytes accessed | tf_op | source)
XLA Modules:
  0.0 83.2 jit_solution(8455022293237944097)
XLA Ops:
  0.6 1.1 %pad_maximum_fusion.own_ref = f32[108,8,128]{2,1,0:T(8,128)S(1)} fusion(f32[12,8,128]{2,1,0:T(8,128)} %bitcast.15, f32[96,8,128]{2,1,0:T(8,128)} %bitcast.13), kind=kLoop, calls=%fused_computation | loop fusion | flops 110592 | bytes 884736 | tf_op jit(solution)/shard_map/concatenate | solution.py:487
  1.7 0.1 pack_rows.1
  1.8 4.0 %collective-permute-start = (f32[54,8,128]{2,1,0:T(8,128)S(1)}, f32[54,8,128]{2,1,0:T(8,128)S(1)}, u32[]{:S(2)}, u32[]{:S(2)}) collective-permute-start(f32[54,8,128]{2,1,0:T(8,128)S(1)} %get-tuple-element.20), channel_id=1, source_target_pairs={{0,16},{16,0},{32,48},{48,32},{64,80},{80,64},{96,112},{112,96},{1... | collective-permute-start | bytes 663560 | tf_op jit(solution)/shard_map/ppermute | solution.py:448
  5.8 14.5 %collective-permute-start.1 = (f32[54,8,128]{2,1,0:T(8,128)S(1)}, f32[54,8,128]{2,1,0:T(8,128)S(1)}, u32[]{:S(2)}, u32[]{:S(2)}) collective-permute-start(f32[54,8,128]{2,1,0:T(8,128)S(1)} %get-tuple-element.21), channel_id=1, source_target_pairs={{496,0},{0,496},{16,32},{32,16},{48,64},{64,48},{80,96},{96,80},{1... | collective-permute-start | bytes 663560 | tf_op jit(solution)/shard_map/ppermute | solution.py:447
  20.3 0.0 copy-start
  20.3 0.7 copy-done
  21.0 0.0 copy-start.1
  21.1 0.7 copy-done.1
  21.8 0.0 copy-start.2
  21.8 0.7 copy-done.2
  22.5 1.8 %weights.1 = (bf16[256,4096]{1,0:T(8,128)(2,1)S(1)}, f32[128,4096]{1,0:T(8,128)S(1)}, f32[8,4096]{1,0:T(8,128)S(1)}, f32[28,8,128]{2,1,0:T(8,128)S(1)}) custom-call(s32[1,4096]{1,0:T(1,128)S(1)} %bitcast.11, f32[2,4096]{1,0:T(2,128)S(1)} %copy-done, f32[1,4096]{1,0:T(1,128)S(1)} %bitcast.12, f32[108,8,128]{2,1,0:T(8,128)S(1)} %pad_maximum_fusion.own_ref), custom_call_target="tpu_custom_call" | custom-call | flops 3000000000 | tf_op jit(solution)/shard_map/weights/pallas_call | solution.py:495
  24.3 0.0 collective-permute-done.got_one
  24.3 0.0 collective-permute-done.1.got_two
  24.3 0.3 pack_cols.1
  24.6 4.7 %collective-permute-start.2 = (f32[7,8,128]{2,1,0:T(8,128)S(1)}, f32[7,8,128]{2,1,0:T(8,128)S(1)}, u32[]{:S(2)}, u32[]{:S(2)}) collective-permute-start(f32[7,8,128]{2,1,0:T(8,128)S(1)} %get-tuple-element.28), channel_id=1, source_target_pairs={{0,1},{1,0},{2,3},{3,2},{4,5},{5,4},{6,7},{7,6},{8,9},{9,8},{10,11... | collective-permute-start | bytes 86024 | tf_op jit(solution)/shard_map/ppermute | solution.py:448
  29.3 2.6 %collective-permute-start.3 = (f32[7,8,128]{2,1,0:T(8,128)S(1)}, f32[7,8,128]{2,1,0:T(8,128)S(1)}, u32[]{:S(2)}, u32[]{:S(2)}) collective-permute-start(f32[7,8,128]{2,1,0:T(8,128)S(1)} %get-tuple-element.29), channel_id=1, source_target_pairs={{15,0},{0,15},{1,2},{2,1},{3,4},{4,3},{5,6},{6,5},{7,8},{8,7},{9,1... | collective-permute-start | bytes 86024 | tf_op jit(solution)/shard_map/ppermute | solution.py:447
  31.9 6.4 %inner.1 = (f32[8,128,128]{2,1,0:T(8,128)S(1)}, f32[28,8,128]{2,1,0:T(8,128)S(1)}, f32[8,4096]{1,0:T(8,128)S(1)}) custom-call(f32[108,16,128]{2,1,0:T(8,128)S(1)} %get-tuple-element.22.ext_ref, bf16[256,4096]{1,0:T(8,128)(2,1)S(1)} %get-tuple-element.23.pick_ref, f32[128,4096]{1,0:T(8,128)S(1)} %get-tuple-element.24.weight_ref), custom_call_target="tpu_custom_call" | custom-call | flops 8000000000 | tf_op jit(solution)/shard_map/inner/pallas_call | solution.py:514
  38.3 0.0 collective-permute-done.2.got_one
  38.3 0.0 collective-permute-done.3.got_two
  38.4 2.3 %edges.1 = (f32[96,8,128]{2,1,0:T(8,128)S(1)}, f32[8,4096]{1,0:T(8,128)S(1)}, f32[1,128]{1,0:T(1,128)S(1)}) custom-call(f32[28,8,128]{2,1,0:T(8,128)S(1)} %get-tuple-element.19.own_ref, f32[8,128,128]{2,1,0:T(8,128)S(1)} %get-tuple-element.25.rows_ref, f32[28,8,128]{2,1,0:T(8,128)S(1)} %get-tuple-element.26.strip_ref, ...), custom_call_target="tpu_custom_call" | custom-call | tf_op jit(solution)/shard_map/edges/pallas_call | solution.py:463
  40.7 22.3 %all_to_all.10 = f32[32,1,128]{2,1,0:T(1,128)S(1)} all-to-all(f32[32,1,128]{2,1,0:T(1,128)S(1)} %broadcast_in_dim.7), channel_id=1, replica_groups=mesh['z_lo'=8,'y'=4,'z_hi'=2,'x'=4,'core'=2] {'y','x','core'}, dimensions={0} | all-to-all | bytes 32768 | tf_op jit(solution)/shard_map/all_to_all | solution.py:459
  63.0 18.9 %all_to_all.11 = f32[16,1,128]{2,1,0:T(1,128)S(1)} all-to-all(f32[16,1,128]{2,1,0:T(1,128)S(1)} %broadcast_in_dim.16), channel_id=1, replica_groups=mesh['z_lo'=8,'y'=4,'z_hi'=2,'x'=4,'core'=2] {'z_lo','z_hi'}, dimensions={0} | all-to-all | bytes 16384 | tf_op jit(solution)/shard_map/all_to_all | solution.py:459
  81.9 1.3 %combine.1 = (f32[96,8,128]{2,1,0:T(8,128)}, f32[8,4096]{1,0:T(8,128)}) custom-call(f32[1,128]{1,0:T(1,128)S(1)} %bitcast.9, f32[96,8,128]{2,1,0:T(8,128)S(1)} %get-tuple-element.32.bred_ref, f32[8,4096]{1,0:T(8,128)S(1)} %get-tuple-element.33.scaled_ref), custom_call_target="tpu_custom_call" | custom-call | tf_op jit(solution)/shard_map/combine/pallas_call | solution.py:524
  (4 shorter events, 0.1 us)
Async XLA Ops:
  1.8 22.5 %collective-permute-start = (f32[54,8,128]{2,1,0:T(8,128)S(1)}, f32[54,8,128]{2,1,0:T(8,128)S(1)}, u32[]{:S(2)}, u32[]{:S(2)}) collective-permute-start(f32[54,8,128]{2,1,0:T(8,128)S(1)} %get-tuple-element.20), channel_id=1, source_target_pairs={{0,16},{16,0},{32,48},{48,32},{64,80},{80,64},{96,112},{112,96},{1... | collective-permute-start | bytes 663560 | tf_op jit(solution)/shard_map/ppermute | solution.py:448
  5.8 18.5 %collective-permute-start.1 = (f32[54,8,128]{2,1,0:T(8,128)S(1)}, f32[54,8,128]{2,1,0:T(8,128)S(1)}, u32[]{:S(2)}, u32[]{:S(2)}) collective-permute-start(f32[54,8,128]{2,1,0:T(8,128)S(1)} %get-tuple-element.21), channel_id=1, source_target_pairs={{496,0},{0,496},{16,32},{32,16},{48,64},{64,48},{80,96},{96,80},{1... | collective-permute-start | bytes 663560 | tf_op jit(solution)/shard_map/ppermute | solution.py:447
  20.3 0.8 copy-start
  21.0 0.7 copy-start.1
  21.8 0.7 copy-start.2
  24.6 13.7 %collective-permute-start.2 = (f32[7,8,128]{2,1,0:T(8,128)S(1)}, f32[7,8,128]{2,1,0:T(8,128)S(1)}, u32[]{:S(2)}, u32[]{:S(2)}) collective-permute-start(f32[7,8,128]{2,1,0:T(8,128)S(1)} %get-tuple-element.28), channel_id=1, source_target_pairs={{0,1},{1,0},{2,3},{3,2},{4,5},{5,4},{6,7},{7,6},{8,9},{9,8},{10,11... | collective-permute-start | bytes 86024 | tf_op jit(solution)/shard_map/ppermute | solution.py:448
  29.3 9.0 %collective-permute-start.3 = (f32[7,8,128]{2,1,0:T(8,128)S(1)}, f32[7,8,128]{2,1,0:T(8,128)S(1)}, u32[]{:S(2)}, u32[]{:S(2)}) collective-permute-start(f32[7,8,128]{2,1,0:T(8,128)S(1)} %get-tuple-element.29), channel_id=1, source_target_pairs={{15,0},{0,15},{1,2},{2,1},{3,4},{4,3},{5,6},{6,5},{7,8},{8,7},{9,1... | collective-permute-start | bytes 86024 | tf_op jit(solution)/shard_map/ppermute | solution.py:447
